TPU v7x, 256 devices: a whole 4x4x8 slice. The times are simulated.
256 devices in a mesh: row: 16 (over y, x), col: 8 (over z), depth: 2 (over core).
Axes of the slice: x: 4, y: 4, z: 8, core: 2. Of those that a mesh axis runs over, the one named last changes fastest.
Arguments:
- matrix_columns: float32 [16, 16, 96, 24576], P(None, ('col', 'depth'), None, 'row'), may hold values from -0.0390625 to 0.0390625
- sources: float32 [16, 16, 96, 128], P('row', ('col', 'depth')), may hold values from -6 to 6
Outputs:
- first_image: float32 [16, 16, 96, 128], P('row', ('col', 'depth'))
- second_image: float32 [16, 16, 96, 128], P('row', ('col', 'depth'))
All inputs are finite; a program needn't handle non-finite values.
Results may differ from a plain program's by a relative error of at most 0.00011.
Values sent between devices are 32-bit elements; how exact they have to be, the bound alone decides.
No kernel may reach another device: no remote copies, remote signals or barrier semaphores. Data moves between devices by JAX's collectives and lax.ppermute only.
A program may use at most 64 MiB of HBM per device.

v0:
```python
import jax
import jax.numpy as jnp
from jax import lax
from jax.sharding import PartitionSpec as P


def copy_for_each(shard, axis):
    copies = jnp.broadcast_to(shard, (lax.axis_size(axis), *shard.shape))
    return lax.all_to_all(copies, axis, split_axis=0, concat_axis=0, tiled=True)


def laid_out(tiles, dim):
    tiles = jnp.moveaxis(tiles, 0, dim)
    lengths = tiles.shape
    return tiles.reshape(*lengths[:dim], lengths[dim] * lengths[dim + 1], *lengths[dim + 2 :])


def collect(shard, axis, dim):
    tiles = copy_for_each(shard, axis)
    return laid_out(tiles, dim)


def cut_along(shard, dim, peers):
    before, after = (shard.shape[:dim], shard.shape[dim + 1 :])
    return jnp.moveaxis(shard.reshape(*before, peers, -1, *after), dim, 0)


def sent_and_summed(shard, axis, dim):
    peers = lax.axis_size(axis)
    tiles = lax.all_to_all(cut_along(shard, dim, peers), axis, 0, 0, tiled=True)
    return jnp.sum(tiles, axis=0)


def contract(window, inputs_flat):
    return lax.dot_general(
        window,
        inputs_flat,
        (((0,), (0,)), ((), ())),
        precision=lax.Precision.HIGHEST,
        preferred_element_type=jnp.float32,
    )


def apply_once(columns, vector_part):
    piece_len = vector_part.shape[2]
    width = vector_part.shape[3]
    gathered = collect(vector_part, "row", 0)
    inputs_flat = gathered.reshape(-1, width)
    owned = sent_and_summed(contract(columns, inputs_flat), ("col", "depth"), 0)
    return owned.reshape(1, 1, piece_len, width)


def body(matrix_columns, sources):
    rows_here = matrix_columns.shape[3]
    columns = matrix_columns.reshape(-1, rows_here)
    first_image = apply_once(columns, sources)
    second_image = apply_once(columns, first_image)
    return (first_image, second_image)


def solution(mesh):
    in_specs = (P(None, ("col", "depth"), None, "row"), P("row", ("col", "depth"), None, None))
    out_specs = (P("row", ("col", "depth"), None, None), P("row", ("col", "depth"), None, None))
    return jax.shard_map(body, mesh=mesh, in_specs=in_specs, out_specs=out_specs, check_vma=False)
```

profile of v0, /device:TPU:1, one launch (start us, length us, event | category | flops | bytes accessed | tf_op | source)
XLA Modules:
  0.0 119.9 jit_solution(9333667525039242)
XLA Ops:
  0.6 1.8 %broadcast_in_dim.6 = f32[16,1,1,96,128]{4,3,2,1,0:T(8,128)} broadcast(f32[96,128]{1,0:T(8,128)} %bitcast.25), dimensions={3,4} | broadcast | bytes 835584 | tf_op jit(solution)/shard_map/broadcast_in_dim | solution.py:8
  2.4 7.6 %all-to-all-start = ((f32[16,1,1,96,128]{4,3,2,1,0:T(8,128)}), f32[16,1,1,96,128]{4,3,2,1,0:T(8,128)S(1)}, u32[]{:S(2)}, u32[]{:S(2)}) async-start(f32[16,1,1,96,128]{4,3,2,1,0:T(8,128)} %broadcast_in_dim.6), calls=%async_computation | async-start | bytes 1572864 | tf_op jit(solution)/shard_map/all_to_all | solution.py:9
  10.0 9.6 %copy.7 = f32[1536,1536]{1,0:T(8,128)} copy(f32[1536,1536]{0,1:T(8,128)} %bitcast.18) | data formatting | bytes 18874368 | tf_op jit(solution)/shard_map/dot_general | solution.py:35
  19.6 3.5 %all-to-all-done = f32[16,1,1,96,128]{4,3,2,1,0:T(8,128)S(1)} async-done(((f32[16,1,1,96,128]{4,3,2,1,0:T(8,128)}), f32[16,1,1,96,128]{4,3,2,1,0:T(8,128)S(1)}, u32[]{:S(2)}, u32[]{:S(2)}) %all-to-all-start) | async-done | bytes 786464 | tf_op jit(solution)/shard_map/all_to_all | solution.py:9
  23.2 10.0 %fusion = f32[16,96,128]{2,1,0:T(8,128)S(1)} fusion(f32[16,96,1536]{2,1,0:T(8,128)} %bitcast.20, f32[1536,128,1]{1,0,2:T(8,128)S(1)} %bitcast.22), kind=kOutput, calls=%fused_computation.1 | convolution fusion | flops 3623878656 | bytes 11010048 | tf_op jit(solution)/shard_map/dot_general | solution.py:35
  33.2 33.5 %all_to_all.20 = f32[16,96,128]{2,1,0:T(8,128)S(1)} all-to-all(f32[16,96,128]{2,1,0:T(8,128)S(1)} %fusion), channel_id=1, replica_groups=mesh['row'=16,'col'=8,'depth'=2] {'col','depth'}, dimensions={0} | all-to-all | bytes 1572864 | tf_op jit(solution)/shard_map/all_to_all | solution.py:30
  66.7 0.0 copy-start
  66.7 0.1 broadcast_in_dim.7
  66.8 17.9 %all_to_all.21 = f32[16,1,1,96,128]{4,3,2,1,0:T(8,128)S(1)} all-to-all(f32[16,1,1,96,128]{4,3,2,1,0:T(8,128)S(1)} %broadcast_in_dim.7), channel_id=1, replica_groups=mesh['row'=16,'col'=8,'depth'=2] {'row'}, dimensions={0} | all-to-all | bytes 1572864 | tf_op jit(solution)/shard_map/all_to_all | solution.py:9
  84.7 8.3 %convolution_bitcast_fusion = f32[1536,128]{0,1:T(8,128)S(1)} fusion(f32[1536,128]{1,0:T(8,128)S(1)} %bitcast.23, f32[1536,1536]{1,0:T(8,128)} %bitcast.19), kind=kOutput, calls=%fused_computation | convolution fusion | flops 3623878656 | bytes 11010048 | tf_op jit(solution)/shard_map/dot_general | solution.py:35
  93.0 0.3 copy.8
  93.2 26.0 %all_to_all.22 = f32[16,96,128]{2,1,0:T(8,128)S(1)} all-to-all(f32[16,96,128]{2,1,0:T(8,128)S(1)} %bitcast.21), channel_id=1, replica_groups=mesh['row'=16,'col'=8,'depth'=2] {'col','depth'}, dimensions={0} | all-to-all | bytes 1572864 | tf_op jit(solution)/shard_map/all_to_all | solution.py:30
  119.3 0.7 reduce_sum.19
  119.9 0.0 copy-done
  (1 shorter events, 0.0 us)
Async XLA Ops:
  2.4 20.8 %all-to-all-start = ((f32[16,1,1,96,128]{4,3,2,1,0:T(8,128)}), f32[16,1,1,96,128]{4,3,2,1,0:T(8,128)S(1)}, u32[]{:S(2)}, u32[]{:S(2)}) async-start(f32[16,1,1,96,128]{4,3,2,1,0:T(8,128)} %broadcast_in_dim.6), calls=%async_computation | async-start | bytes 1572864 | tf_op jit(solution)/shard_map/all_to_all | solution.py:9
  66.7 53.2 %copy-start = (f32[96,128]{1,0:T(8,128)}, f32[96,128]{1,0:T(8,128)S(1)}, u32[]{:S(2)}) copy-start(f32[96,128]{1,0:T(8,128)S(1)} %reduce_sum.18) | copy-start | bytes 147460
where the time goes:
time: 120 us
  blocking collectives  77.4 us (65%)
  matrix products  18.3 us (15%)
  local copies, waits for them, and re-layouts  11.7 us (10%)
  starting transfers between devices  7.58 us (6%)
  waiting for transfers between devices  3.54 us (3%)
    all_to_all x2, blocking collectives, sent_and_summed(): tiles = lax.all_to_all(cut_along(shard, dim, peers), axis, 0, 0, tiled=True)  59.5 us
    dot_general x2, matrix products, contract(): lax.dot_general(window, inputs_flat, (((0,), (0,)), ((), ())), precision=...  18.3 us
    all_to_all x1, blocking collectives, copy_for_each(): return lax.all_to_all(copies, axis, split_axis=0, concat_axis=0, tiled=True)  17.9 us
    dot_general x2, local copies, waits for them, and re-layouts, contract(): lax.dot_general(window, inputs_flat, (((0,), (0,)), ((), ())), precision=...  9.9 us
    all_to_all x1, starting transfers between devices, copy_for_each(): return lax.all_to_all(copies, axis, split_axis=0, concat_axis=0, tiled=True)  7.58 us
    all_to_all x1, waiting for transfers between devices, copy_for_each(): return lax.all_to_all(copies, axis, split_axis=0, concat_axis=0, tiled=True)  3.54 us
  transfers between devices with their start and end apart: 1, of which 1 were waited for; matrix products, arithmetic and copies ran while one was open for 8% of the time, Pallas kernels for 0%

commit v1 on v0

v1 whole, which is shorter than its diff:
```python
import functools

import jax
import jax.numpy as jnp
from jax import lax
from jax.experimental import pallas as pl
from jax.experimental.pallas import tpu as pltpu
from jax.sharding import PartitionSpec as P

ROUND = 4
CHUNKS = 3
DIRECT = True
VMEM_LIMIT = 40 * 2**20
SMALL_LIMIT = 10 * 2**20


def split_kernel(slot_ref, matrix_hbm, high_hbm, low_hbm, matrix_ref, high_ref, low_ref, in_sems, out_sems, *, piece):
    width = ROUND * piece
    rounds = matrix_ref.shape[1] // width
    arriving = []
    for i in range(rounds):
        at = pl.ds(i * width, width)
        copy = pltpu.make_async_copy(matrix_hbm.at[:, at], matrix_ref.at[:, at], in_sems.at[i])
        copy.start()
        arriving.append(copy)
    leaving = []
    for i in range(rounds):
        arriving[i].wait()
        turned = matrix_ref[:, i * width : (i + 1) * width].T
        for k in range(ROUND):
            n = i * ROUND + k
            rows = turned[k * piece : (k + 1) * piece]
            high = rows.astype(jnp.bfloat16)
            at = pl.ds(n * piece, piece)
            high_ref[at, :] = high
            low_ref[at, :] = (rows - high.astype(jnp.float32)).astype(jnp.bfloat16)
            there = pl.ds(pl.multiple_of(slot_ref[n] * piece, piece), piece)
            for j, (here, far) in enumerate(((high_ref, high_hbm), (low_ref, low_hbm))):
                copy = pltpu.make_async_copy(here.at[at], far.at[there], out_sems.at[j, n])
                copy.start()
                leaving.append(copy)
    for copy in leaving:
        copy.wait()


def split_matrix(slots, columns, piece):
    depth, rows = columns.shape
    far = pl.BlockSpec(memory_space=pltpu.HBM)
    out = pltpu.HBM((rows, depth), jnp.bfloat16)
    held = pltpu.VMEM((rows, depth), jnp.bfloat16)
    return pl.pallas_call(
        functools.partial(split_kernel, piece=piece),
        in_specs=[pl.BlockSpec(memory_space=pltpu.SMEM), far],
        out_specs=[far, far],
        out_shape=[out, out],
        scratch_shapes=[
            pltpu.VMEM((depth, rows), jnp.float32),
            held,
            held,
            pltpu.SemaphoreType.DMA((rows // (ROUND * piece),)),
            pltpu.SemaphoreType.DMA((2, rows // piece)),
        ],
        compiler_params=pltpu.CompilerParams(vmem_limit_bytes=VMEM_LIMIT),
        name="split_matrix",
    )(slots, pltpu.with_memory_space_constraint(columns, pltpu.HBM))


def halves_of(vectors):
    top = vectors.astype(jnp.bfloat16)
    rest = (vectors - top.astype(jnp.float32)).astype(jnp.bfloat16)
    return top, jnp.concatenate([top, rest], axis=1)


def multiply(high, low, top, both):
    width = top.shape[1]
    main = jnp.dot(high, both, preferred_element_type=jnp.float32)
    small = jnp.dot(low, top, preferred_element_type=jnp.float32)
    return main[:, :width] + (main[:, width:] + small)


def streamed_kernel(high_hbm, low_hbm, vectors_ref, out_ref, high_ref, low_ref, sems, *, start):
    rows = high_ref.shape[0]
    step = rows // CHUNKS
    copies = []
    for k in range(CHUNKS):
        at = pl.ds(k * step, step)
        there = pl.ds(start + k * step, step)
        pair = [
            pltpu.make_async_copy(high_hbm.at[there], high_ref.at[at], sems.at[0, k]),
            pltpu.make_async_copy(low_hbm.at[there], low_ref.at[at], sems.at[1, k]),
        ]
        for copy in pair:
            copy.start()
        copies.append(pair)
    top, both = halves_of(vectors_ref[...])
    for k in range(CHUNKS):
        for copy in copies[k]:
            copy.wait()
        at = pl.ds(k * step, step)
        out_ref[at, :] = multiply(high_ref[at, :], low_ref[at, :], top, both)


def product_streamed(high, low, vectors, half):
    rows, depth = high.shape
    width = vectors.shape[1]
    rows //= 2
    on_chip = pl.BlockSpec(memory_space=pltpu.VMEM)
    far = pl.BlockSpec(memory_space=pltpu.HBM)
    held = pltpu.VMEM((rows, depth), jnp.bfloat16)
    return pl.pallas_call(
        functools.partial(streamed_kernel, start=half * rows),
        in_specs=[far, far, on_chip],
        out_specs=[on_chip, on_chip, on_chip],
        out_shape=[jax.ShapeDtypeStruct((rows, width), jnp.float32), held, held],
        scratch_shapes=[pltpu.SemaphoreType.DMA((2, CHUNKS))],
        compiler_params=pltpu.CompilerParams(vmem_limit_bytes=SMALL_LIMIT),
        name="product_streamed",
    )(*(pltpu.with_memory_space_constraint(m, pltpu.HBM) for m in (high, low)), vectors)


def product_kernel(high_ref, low_ref, vectors_ref, out_ref):
    top, both = halves_of(vectors_ref[...])
    out_ref[...] = multiply(high_ref[...], low_ref[...], top, both)


def product(high, low, vectors):
    on_chip = pl.BlockSpec(memory_space=pltpu.VMEM)
    return pl.pallas_call(
        product_kernel,
        in_specs=[on_chip, on_chip, on_chip],
        out_specs=on_chip,
        out_shape=jax.ShapeDtypeStruct((high.shape[0], vectors.shape[1]), jnp.float32),
        compiler_params=pltpu.CompilerParams(vmem_limit_bytes=SMALL_LIMIT),
        name="product",
    )(high, low, vectors)


def gather_rows(part):
    copies = jnp.broadcast_to(part, (lax.axis_size("row"), *part.shape))
    return lax.all_to_all(copies, "row", split_axis=0, concat_axis=0, tiled=True)


def slots_here(direct):
    ring = lax.axis_size("col")
    core, place = lax.axis_index("depth"), lax.axis_index("col")
    owner = jnp.arange(2 * ring, dtype=jnp.int32)
    chip, owner_core = owner // 2, owner % 2
    if not direct:
        return jnp.where(owner_core == core, 0, ring) + chip
    ahead = jnp.remainder(chip - place, ring)
    half = ring // 2
    before = ahead > half
    hops = jnp.where(before, ring - ahead, ahead)
    shared = (ahead == 0) | (ahead == half)
    handler = jnp.where(shared, owner_core, before.astype(jnp.int32))
    slot = jnp.where(shared, jnp.where(ahead == 0, ring - 1, ring - 2), 2 * (hops - 1) + owner_core)
    return (jnp.where(handler == core, 0, ring) + slot).astype(jnp.int32)


SWAP = [(0, 1), (1, 0)]


def to_owners(ours, theirs, core_row, piece):
    width = ours.shape[-1]
    ring = lax.axis_size("col")
    received = lax.ppermute(theirs, "depth", SWAP)
    summed = (ours + received).reshape(-1, piece, width)
    if not DIRECT:
        tiles = lax.all_to_all(summed, "col", 0, 0, tiled=True)
        return jnp.sum(tiles, axis=0)
    axes = ("col", "depth")

    def pairs(hops):
        return [(2 * z + c, 2 * ((z + (1 - 2 * c) * hops) % ring) + c) for z in range(ring) for c in range(2)]

    half = ring // 2
    arrived = []
    for hops in range(1, half):
        arrived.append(lax.ppermute(summed[2 * (hops - 1) : 2 * hops], axes, pairs(hops)))
    opposite = lax.ppermute(summed[ring - 2], axes, pairs(half))
    both = sum(arrived[1:], arrived[0])
    first_core = core_row == 0
    give = jnp.where(first_core, both[1], both[0])
    keep = jnp.where(first_core, both[0], both[1])
    last = lax.ppermute(give, "depth", SWAP)
    return summed[ring - 1] + opposite + keep + last


def body(matrix_columns, sources):
    rows_here = matrix_columns.shape[3]
    piece, width = sources.shape[2:]
    gathered = gather_rows(sources.reshape(piece, width)).reshape(-1, width)
    core_row = lax.optimization_barrier(jnp.broadcast_to(lax.axis_index("depth"), (1, width)))
    high, low = split_matrix(slots_here(DIRECT), matrix_columns.reshape(-1, rows_here), piece)
    theirs, their_high, their_low = product_streamed(high, low, gathered, 1)
    ours, our_high, our_low = product_streamed(high, low, gathered, 0)
    first = to_owners(ours, theirs, core_row, piece)
    gathered = gather_rows(first).reshape(-1, width)
    theirs = product(their_high, their_low, gathered)
    ours = product(our_high, our_low, gathered)
    second = to_owners(ours, theirs, core_row, piece)
    return first.reshape(sources.shape), second.reshape(sources.shape)


def solution(mesh):
    in_specs = (P(None, ("col", "depth"), None, "row"), P("row", ("col", "depth"), None, None))
    out_specs = (P("row", ("col", "depth"), None, None), P("row", ("col", "depth"), None, None))
    return jax.shard_map(body, mesh=mesh, in_specs=in_specs, out_specs=out_specs, check_vma=False)
```

time: 120 us -> 85.6 us (0.71)
  blocking collectives: 77.4 us -> 16.1 us
  starting transfers between devices: 7.58 us -> 34 us
  matrix products: 18.3 us -> 0 us
  Pallas kernels: 0 us -> 17.1 us
  waiting for transfers between devices: 3.54 us -> 14.6 us
  local copies, waits for them, and re-layouts: 11.7 us -> 1.87 us
    all_to_all x3 -> x1, blocking collectives: 77.4 us -> 16.1 us  [gather_rows(): lax.all_to_all(copies, 'row', split_axis=0, concat_axis=0, tiled=True)]
    ppermute x0 -> x12, starting transfers between devices: none -> 26.4 us  [the longest x6 11.9 us: to_owners(): lax.ppermute(summed[2 * (hops - 1):2 * hops], axes, pairs(hops))]
    dot_general x2 -> x0, matrix products: 18.3 us -> none  [contract(): lax.dot_general(window, inputs_flat, (((0,), (0,)), ((), ())), precision=...]
    pallas_call x0 -> x5, Pallas kernels: none -> 17.1 us  [the longest x1 7.94 us: split_matrix(): pl.pallas_call(functools.partial(split_kernel, piece=piece), in_specs=[pl...]
    dot_general x2 -> x0, local copies, waits for them, and re-layouts: 9.9 us -> none  [contract(): lax.dot_general(window, inputs_flat, (((0,), (0,)), ((), ())), precision=...]
    ppermute x0 -> x12, waiting for transfers between devices: none -> 9.42 us  [the longest x6 7.66 us: to_owners(): lax.ppermute(summed[2 * (hops - 1):2 * hops], axes, pairs(hops))]
    all_to_all x1, waiting for transfers between devices: 3.54 us -> 5.2 us  [gather_rows(): lax.all_to_all(copies, 'row', split_axis=0, concat_axis=0, tiled=True)]
  transfers between devices with their start and end apart: 1 -> 13, of which waited for: 1 -> 8; matrix products, arithmetic and copies ran while one was open for 8% -> 0% of each run, Pallas kernels for 0% -> 15%
where the time goes in v1:
time: 85.6 us; the launch traced here: 85.3 us
  starting transfers between devices  34 us (40%)
  Pallas kernels  17.1 us (20%)
  blocking collectives  16.1 us (19%)
  waiting for transfers between devices  14.6 us (17%)
  local copies, waits for them, and re-layouts  1.87 us (2%)
    all_to_all x1, blocking collectives, gather_rows(): lax.all_to_all(copies, 'row', split_axis=0, concat_axis=0, tiled=True)  16.1 us
    ppermute x6, starting transfers between devices, to_owners(): lax.ppermute(summed[2 * (hops - 1):2 * hops], axes, pairs(hops))  11.9 us
    pallas_call x1, Pallas kernels, split_matrix(): pl.pallas_call(functools.partial(split_kernel, piece=piece), in_specs=[pl...  7.94 us
    ppermute x6, waiting for transfers between devices, to_owners(): lax.ppermute(summed[2 * (hops - 1):2 * hops], axes, pairs(hops))  7.66 us
    all_to_all x1, starting transfers between devices, gather_rows(): lax.all_to_all(copies, 'row', split_axis=0, concat_axis=0, tiled=True)  7.58 us
    ppermute x2, starting transfers between devices, to_owners(): opposite = lax.ppermute(summed[ring - 2], axes, pairs(half))  7.39 us
    pallas_call x2, Pallas kernels, product_streamed(): pl.pallas_call(functools.partial(streamed_kernel, start=half * rows), in_...  6.36 us
    all_to_all x1, waiting for transfers between devices, gather_rows(): lax.all_to_all(copies, 'row', split_axis=0, concat_axis=0, tiled=True)  5.2 us
  transfers between devices with their start and end apart: 13, of which 8 were waited for; matrix products, arithmetic and copies ran while one was open for 0% of the time, Pallas kernels for 15%

profile of v1, /device:TPU:1, one launch (start us, length us, event | category | flops | bytes accessed | tf_op | source)
XLA Modules:
  0.0 85.3 jit_solution(17043705703428992497)
XLA Ops:
  0.6 1.7 %broadcast_in_dim.37 = f32[16,96,128]{2,1,0:T(8,128)} broadcast(f32[96,128]{1,0:T(8,128)} %bitcast.51), dimensions={1,2} | broadcast | bytes 835584 | tf_op jit(solution)/shard_map/broadcast_in_dim | solution.py:139
  2.4 7.6 %all-to-all-start = ((f32[16,96,128]{2,1,0:T(8,128)}), f32[16,96,128]{2,1,0:T(8,128)S(1)}, u32[]{:S(2)}, u32[]{:S(2)}) async-start(f32[16,96,128]{2,1,0:T(8,128)} %broadcast_in_dim.37), calls=%async_computation | async-start | bytes 1572864 | tf_op jit(solution)/shard_map/all_to_all | solution.py:140
  10.0 7.9 %split_matrix.1 = (bf16[1536,1536]{1,0:T(8,128)(2,1)}, bf16[1536,1536]{1,0:T(8,128)(2,1)}) custom-call(s32[16]{0:T(128)S(1)} %fusion.9.slot_ref, f32[1536,1536]{1,0:T(8,128)} %bitcast.43), custom_call_target="tpu_custom_call" | custom-call | tf_op jit(solution)/shard_map/split_matrix/pallas_call | solution.py:51
  17.9 5.2 %all-to-all-done = f32[16,96,128]{2,1,0:T(8,128)S(1)} async-done(((f32[16,96,128]{2,1,0:T(8,128)}), f32[16,96,128]{2,1,0:T(8,128)S(1)}, u32[]{:S(2)}, u32[]{:S(2)}) %all-to-all-start) | async-done | bytes 786464 | tf_op jit(solution)/shard_map/all_to_all | solution.py:140
  23.1 3.2 %product_streamed.3 = (f32[768,128]{1,0:T(8,128)S(1)}, bf16[768,1536]{1,0:T(8,128)(2,1)S(1)}, bf16[768,1536]{1,0:T(8,128)(2,1)S(1)}) custom-call(bf16[1536,1536]{1,0:T(8,128)(2,1)} %get-tuple-element.10.high_hbm, bf16[1536,1536]{1,0:T(8,128)(2,1)} %get-tuple-element.11.low_hbm, f32[1536,128]{1,0:T(8,128)S(1)} %bitcast.39), custom_call_target="tpu_custom_call" | custom-call | tf_op jit(solution)/shard_map/product_streamed/pallas_call | solution.py:110
  26.3 2.4 %collective-permute-start = (f32[768,128]{1,0:T(8,128)S(1)}, f32[768,128]{1,0:T(8,128)S(1)}, u32[]{:S(2)}, u32[]{:S(2)}) collective-permute-start(f32[768,128]{1,0:T(8,128)S(1)} %get-tuple-element.13), channel_id=1, source_target_pairs={{0,1},{1,0},{2,3},{3,2},{4,5},{5,4},{6,7},{7,6},{8,9},{9,8},{10,11... | collective-permute-start | bytes 1179656 | tf_op jit(solution)/shard_map/ppermute | solution.py:166
  28.7 3.2 %product_streamed.2 = (f32[768,128]{1,0:T(8,128)S(1)}, bf16[768,1536]{1,0:T(8,128)(2,1)S(1)}, bf16[768,1536]{1,0:T(8,128)(2,1)S(1)}) custom-call(bf16[1536,1536]{1,0:T(8,128)(2,1)} %get-tuple-element.10.high_hbm, bf16[1536,1536]{1,0:T(8,128)(2,1)} %get-tuple-element.11.low_hbm, f32[1536,128]{1,0:T(8,128)S(1)} %bitcast.40), custom_call_target="tpu_custom_call" | custom-call | tf_op jit(solution)/shard_map/product_streamed/pallas_call | solution.py:110
  31.9 0.0 collective-permute-done
  32.0 6.5 %collective-permute-start.4 = (f32[2,96,128]{2,1,0:T(8,128)S(1)}, f32[2,96,128]{2,1,0:T(8,128)S(1)}, u32[]{:S(2)}, u32[]{:S(2)}) collective-permute-start(f32[2,96,128]{2,1,0:T(8,128)S(1)} %bitcast.49), channel_id=1, source_target_pairs={{0,6},{1,11},{2,8},{3,13},{4,10},{5,15},{6,12},{7,1},{8,14},{9,3},... | collective-permute-start | bytes 294920 | tf_op jit(solution)/shard_map/ppermute | solution.py:179
  38.5 0.3 collective-permute-start.3
  38.8 0.5 collective-permute-start.2
  39.3 4.6 %collective-permute-start.1 = (f32[96,128]{1,0:T(8,128)S(1)}, f32[96,128]{1,0:T(8,128)S(1)}, u32[]{:S(2)}, u32[]{:S(2)}) collective-permute-start(f32[96,128]{1,0:T(8,128)S(1)} %slice.89), channel_id=1, source_target_pairs={{0,8},{1,9},{2,10},{3,11},{4,12},{5,13},{6,14},{7,15},{8,0},{9,1},... | collective-permute-start | bytes 147464 | tf_op jit(solution)/shard_map/ppermute | solution.py:180
  43.8 0.0 collective-permute-done.4
  43.8 0.9 %collective-permute-done.3 = f32[2,96,128]{2,1,0:T(8,128)S(1)} collective-permute-done((f32[2,96,128]{2,1,0:T(8,128)S(1)}, f32[2,96,128]{2,1,0:T(8,128)S(1)}, u32[]{:S(2)}, u32[]{:S(2)}) %collective-permute-start.3) | collective-permute-done | bytes 98336 | tf_op jit(solution)/shard_map/ppermute | solution.py:179
  44.7 2.2 %collective-permute-done.2 = f32[2,96,128]{2,1,0:T(8,128)S(1)} collective-permute-done((f32[2,96,128]{2,1,0:T(8,128)S(1)}, f32[2,96,128]{2,1,0:T(8,128)S(1)}, u32[]{:S(2)}, u32[]{:S(2)}) %collective-permute-start.2) | collective-permute-done | bytes 98336 | tf_op jit(solution)/shard_map/ppermute | solution.py:179
  47.0 1.9 %collective-permute-start.5 = (f32[96,128]{1,0:T(8,128)S(1)}, f32[96,128]{1,0:T(8,128)S(1)}, u32[]{:S(2)}, u32[]{:S(2)}) collective-permute-start(f32[96,128]{1,0:T(8,128)S(1)} %fusion.5), channel_id=1, source_target_pairs={{0,1},{1,0},{2,3},{3,2},{4,5},{5,4},{6,7},{7,6},{8,9},{9,8},{10,11... | collective-permute-start | bytes 147464 | tf_op jit(solution)/shard_map/ppermute | solution.py:185
  48.9 0.0 collective-permute-done.1
  48.9 0.9 %collective-permute-done.5 = f32[96,128]{1,0:T(8,128)S(1)} collective-permute-done((f32[96,128]{1,0:T(8,128)S(1)}, f32[96,128]{1,0:T(8,128)S(1)}, u32[]{:S(2)}, u32[]{:S(2)}) %collective-permute-start.5) | collective-permute-done | bytes 49184 | tf_op jit(solution)/shard_map/ppermute | solution.py:185
  49.8 0.0 copy-start
  49.8 0.1 broadcast_in_dim.41
  49.9 16.1 %all_to_all.10 = f32[16,96,128]{2,1,0:T(8,128)S(1)} all-to-all(f32[16,96,128]{2,1,0:T(8,128)S(1)} %broadcast_in_dim.41), channel_id=1, replica_groups=mesh['row'=16,'col'=8,'depth'=2] {'row'}, dimensions={0} | all-to-all | bytes 1572864 | tf_op jit(solution)/shard_map/all_to_all | solution.py:140
  66.0 1.4 %product.3 = f32[768,128]{1,0:T(8,128)S(1)} custom-call(bf16[768,1536]{1,0:T(8,128)(2,1)S(1)} %get-tuple-element.16.high_ref, bf16[768,1536]{1,0:T(8,128)(2,1)S(1)} %get-tuple-element.17.low_ref, f32[1536,128]{1,0:T(8,128)S(1)} %bitcast.41), custom_call_target="tpu_custom_call" | custom-call | tf_op jit(solution)/shard_map/product/pallas_call | solution.py:128
  67.4 0.0 copy-done
  67.4 1.9 %collective-permute-start.6 = (f32[768,128]{1,0:T(8,128)S(1)}, f32[768,128]{1,0:T(8,128)S(1)}, u32[]{:S(2)}, u32[]{:S(2)}) collective-permute-start(f32[768,128]{1,0:T(8,128)S(1)} %product.3), channel_id=1, source_target_pairs={{0,1},{1,0},{2,3},{3,2},{4,5},{5,4},{6,7},{7,6},{8,9},{9,8},{10,11... | collective-permute-start | bytes 1179656 | tf_op jit(solution)/shard_map/ppermute | solution.py:166
  69.3 1.4 %product.2 = f32[768,128]{1,0:T(8,128)S(1)} custom-call(bf16[768,1536]{1,0:T(8,128)(2,1)S(1)} %get-tuple-element.14.high_ref, bf16[768,1536]{1,0:T(8,128)(2,1)S(1)} %get-tuple-element.15.low_ref, f32[1536,128]{1,0:T(8,128)S(1)} %bitcast.42), custom_call_target="tpu_custom_call" | custom-call | tf_op jit(solution)/shard_map/product/pallas_call | solution.py:128
  70.7 0.0 collective-permute-done.6
  70.8 2.0 %collective-permute-start.10 = (f32[2,96,128]{2,1,0:T(8,128)S(1)}, f32[2,96,128]{2,1,0:T(8,128)S(1)}, u32[]{:S(2)}, u32[]{:S(2)}) collective-permute-start(f32[2,96,128]{2,1,0:T(8,128)S(1)} %bitcast.50), channel_id=1, source_target_pairs={{0,6},{1,11},{2,8},{3,13},{4,10},{5,15},{6,12},{7,1},{8,14},{9,3},... | collective-permute-start | bytes 294920 | tf_op jit(solution)/shard_map/ppermute | solution.py:179
  72.7 2.0 %collective-permute-start.9 = (f32[2,96,128]{2,1,0:T(8,128)S(1)}, f32[2,96,128]{2,1,0:T(8,128)S(1)}, u32[]{:S(2)}, u32[]{:S(2)}) collective-permute-start(f32[2,96,128]{2,1,0:T(8,128)S(1)} %bitcast.48), channel_id=1, source_target_pairs={{0,4},{1,13},{2,6},{3,15},{4,8},{5,1},{6,10},{7,3},{8,12},{9,5},{1... | collective-permute-start | bytes 294920 | tf_op jit(solution)/shard_map/ppermute | solution.py:179
  74.8 0.6 collective-permute-start.8
  75.4 2.8 %collective-permute-start.7 = (f32[96,128]{1,0:T(8,128)S(1)}, f32[96,128]{1,0:T(8,128)S(1)}, u32[]{:S(2)}, u32[]{:S(2)}) collective-permute-start(f32[96,128]{1,0:T(8,128)S(1)} %slice.96), channel_id=1, source_target_pairs={{0,8},{1,9},{2,10},{3,11},{4,12},{5,13},{6,14},{7,15},{8,0},{9,1},... | collective-permute-start | bytes 147464 | tf_op jit(solution)/shard_map/ppermute | solution.py:180
  78.2 0.3 collective-permute-done.10
  78.5 2.3 %collective-permute-done.9 = f32[2,96,128]{2,1,0:T(8,128)S(1)} collective-permute-done((f32[2,96,128]{2,1,0:T(8,128)S(1)}, f32[2,96,128]{2,1,0:T(8,128)S(1)}, u32[]{:S(2)}, u32[]{:S(2)}) %collective-permute-start.9) | collective-permute-done | bytes 98336 | tf_op jit(solution)/shard_map/ppermute | solution.py:179
  80.9 1.9 %collective-permute-done.8 = f32[2,96,128]{2,1,0:T(8,128)S(1)} collective-permute-done((f32[2,96,128]{2,1,0:T(8,128)S(1)}, f32[2,96,128]{2,1,0:T(8,128)S(1)}, u32[]{:S(2)}, u32[]{:S(2)}) %collective-permute-start.8) | collective-permute-done | bytes 98336 | tf_op jit(solution)/shard_map/ppermute | solution.py:179
  82.8 1.0 %collective-permute-start.11 = (f32[96,128]{1,0:T(8,128)S(1)}, f32[96,128]{1,0:T(8,128)S(1)}, u32[]{:S(2)}, u32[]{:S(2)}) collective-permute-start(f32[96,128]{1,0:T(8,128)S(1)} %fusion.6), channel_id=1, source_target_pairs={{0,1},{1,0},{2,3},{3,2},{4,5},{5,4},{6,7},{7,6},{8,9},{9,8},{10,11... | collective-permute-start | bytes 147464 | tf_op jit(solution)/shard_map/ppermute | solution.py:185
  83.8 0.0 collective-permute-done.7
  83.8 0.9 %collective-permute-done.11 = f32[96,128]{1,0:T(8,128)S(1)} collective-permute-done((f32[96,128]{1,0:T(8,128)S(1)}, f32[96,128]{1,0:T(8,128)S(1)}, u32[]{:S(2)}, u32[]{:S(2)}) %collective-permute-start.11) | collective-permute-done | bytes 49184 | tf_op jit(solution)/shard_map/ppermute | solution.py:185
  84.7 0.6 fusion.2
  (14 shorter events, 0.2 us)
Async XLA Ops:
  2.4 20.8 %all-to-all-start = ((f32[16,96,128]{2,1,0:T(8,128)}), f32[16,96,128]{2,1,0:T(8,128)S(1)}, u32[]{:S(2)}, u32[]{:S(2)}) async-start(f32[16,96,128]{2,1,0:T(8,128)} %broadcast_in_dim.37), calls=%async_computation | async-start | bytes 1572864 | tf_op jit(solution)/shard_map/all_to_all | solution.py:140
  26.3 5.6 %collective-permute-start = (f32[768,128]{1,0:T(8,128)S(1)}, f32[768,128]{1,0:T(8,128)S(1)}, u32[]{:S(2)}, u32[]{:S(2)}) collective-permute-start(f32[768,128]{1,0:T(8,128)S(1)} %get-tuple-element.13), channel_id=1, source_target_pairs={{0,1},{1,0},{2,3},{3,2},{4,5},{5,4},{6,7},{7,6},{8,9},{9,8},{10,11... | collective-permute-start | bytes 1179656 | tf_op jit(solution)/shard_map/ppermute | solution.py:166
  32.0 11.9 %collective-permute-start.4 = (f32[2,96,128]{2,1,0:T(8,128)S(1)}, f32[2,96,128]{2,1,0:T(8,128)S(1)}, u32[]{:S(2)}, u32[]{:S(2)}) collective-permute-start(f32[2,96,128]{2,1,0:T(8,128)S(1)} %bitcast.49), channel_id=1, source_target_pairs={{0,6},{1,11},{2,8},{3,13},{4,10},{5,15},{6,12},{7,1},{8,14},{9,3},... | collective-permute-start | bytes 294920 | tf_op jit(solution)/shard_map/ppermute | solution.py:179
  38.5 6.2 %collective-permute-start.3 = (f32[2,96,128]{2,1,0:T(8,128)S(1)}, f32[2,96,128]{2,1,0:T(8,128)S(1)}, u32[]{:S(2)}, u32[]{:S(2)}) collective-permute-start(f32[2,96,128]{2,1,0:T(8,128)S(1)} %bitcast.47), channel_id=1, source_target_pairs={{0,4},{1,13},{2,6},{3,15},{4,8},{5,1},{6,10},{7,3},{8,12},{9,5},{1... | collective-permute-start | bytes 294920 | tf_op jit(solution)/shard_map/ppermute | solution.py:179
  38.8 8.1 %collective-permute-start.2 = (f32[2,96,128]{2,1,0:T(8,128)S(1)}, f32[2,96,128]{2,1,0:T(8,128)S(1)}, u32[]{:S(2)}, u32[]{:S(2)}) collective-permute-start(f32[2,96,128]{2,1,0:T(8,128)S(1)} %bitcast.45), channel_id=1, source_target_pairs={{0,2},{1,15},{2,4},{3,1},{4,6},{5,3},{6,8},{7,5},{8,10},{9,7},{10,... | collective-permute-start | bytes 294920 | tf_op jit(solution)/shard_map/ppermute | solution.py:179
  39.3 9.6 %collective-permute-start.1 = (f32[96,128]{1,0:T(8,128)S(1)}, f32[96,128]{1,0:T(8,128)S(1)}, u32[]{:S(2)}, u32[]{:S(2)}) collective-permute-start(f32[96,128]{1,0:T(8,128)S(1)} %slice.89), channel_id=1, source_target_pairs={{0,8},{1,9},{2,10},{3,11},{4,12},{5,13},{6,14},{7,15},{8,0},{9,1},... | collective-permute-start | bytes 147464 | tf_op jit(solution)/shard_map/ppermute | solution.py:180
  47.0 2.8 %collective-permute-start.5 = (f32[96,128]{1,0:T(8,128)S(1)}, f32[96,128]{1,0:T(8,128)S(1)}, u32[]{:S(2)}, u32[]{:S(2)}) collective-permute-start(f32[96,128]{1,0:T(8,128)S(1)} %fusion.5), channel_id=1, source_target_pairs={{0,1},{1,0},{2,3},{3,2},{4,5},{5,4},{6,7},{7,6},{8,9},{9,8},{10,11... | collective-permute-start | bytes 147464 | tf_op jit(solution)/shard_map/ppermute | solution.py:185
  49.8 17.6 %copy-start = (f32[96,128]{1,0:T(8,128)}, f32[96,128]{1,0:T(8,128)S(1)}, u32[]{:S(2)}) copy-start(f32[96,128]{1,0:T(8,128)S(1)} %fusion.4) | copy-start | bytes 147460
  67.4 3.3 %collective-permute-start.6 = (f32[768,128]{1,0:T(8,128)S(1)}, f32[768,128]{1,0:T(8,128)S(1)}, u32[]{:S(2)}, u32[]{:S(2)}) collective-permute-start(f32[768,128]{1,0:T(8,128)S(1)} %product.3), channel_id=1, source_target_pairs={{0,1},{1,0},{2,3},{3,2},{4,5},{5,4},{6,7},{7,6},{8,9},{9,8},{10,11... | collective-permute-start | bytes 1179656 | tf_op jit(solution)/shard_map/ppermute | solution.py:166
  70.8 7.8 %collective-permute-start.10 = (f32[2,96,128]{2,1,0:T(8,128)S(1)}, f32[2,96,128]{2,1,0:T(8,128)S(1)}, u32[]{:S(2)}, u32[]{:S(2)}) collective-permute-start(f32[2,96,128]{2,1,0:T(8,128)S(1)} %bitcast.50), channel_id=1, source_target_pairs={{0,6},{1,11},{2,8},{3,13},{4,10},{5,15},{6,12},{7,1},{8,14},{9,3},... | collective-permute-start | bytes 294920 | tf_op jit(solution)/shard_map/ppermute | solution.py:179
  72.7 8.1 %collective-permute-start.9 = (f32[2,96,128]{2,1,0:T(8,128)S(1)}, f32[2,96,128]{2,1,0:T(8,128)S(1)}, u32[]{:S(2)}, u32[]{:S(2)}) collective-permute-start(f32[2,96,128]{2,1,0:T(8,128)S(1)} %bitcast.48), channel_id=1, source_target_pairs={{0,4},{1,13},{2,6},{3,15},{4,8},{5,1},{6,10},{7,3},{8,12},{9,5},{1... | collective-permute-start | bytes 294920 | tf_op jit(solution)/shard_map/ppermute | solution.py:179
  74.8 8.0 %collective-permute-start.8 = (f32[2,96,128]{2,1,0:T(8,128)S(1)}, f32[2,96,128]{2,1,0:T(8,128)S(1)}, u32[]{:S(2)}, u32[]{:S(2)}) collective-permute-start(f32[2,96,128]{2,1,0:T(8,128)S(1)} %bitcast.46), channel_id=1, source_target_pairs={{0,2},{1,15},{2,4},{3,1},{4,6},{5,3},{6,8},{7,5},{8,10},{9,7},{10,... | collective-permute-start | bytes 294920 | tf_op jit(solution)/shard_map/ppermute | solution.py:179
  75.4 8.4 %collective-permute-start.7 = (f32[96,128]{1,0:T(8,128)S(1)}, f32[96,128]{1,0:T(8,128)S(1)}, u32[]{:S(2)}, u32[]{:S(2)}) collective-permute-start(f32[96,128]{1,0:T(8,128)S(1)} %slice.96), channel_id=1, source_target_pairs={{0,8},{1,9},{2,10},{3,11},{4,12},{5,13},{6,14},{7,15},{8,0},{9,1},... | collective-permute-start | bytes 147464 | tf_op jit(solution)/shard_map/ppermute | solution.py:180
  82.8 1.8 %collective-permute-start.11 = (f32[96,128]{1,0:T(8,128)S(1)}, f32[96,128]{1,0:T(8,128)S(1)}, u32[]{:S(2)}, u32[]{:S(2)}) collective-permute-start(f32[96,128]{1,0:T(8,128)S(1)} %fusion.6), channel_id=1, source_target_pairs={{0,1},{1,0},{2,3},{3,2},{4,5},{5,4},{6,7},{7,6},{8,9},{9,8},{10,11... | collective-permute-start | bytes 147464 | tf_op jit(solution)/shard_map/ppermute | solution.py:185

commit v2 on v0

v2 whole, which is shorter than its diff:
```python
import functools

import jax
import jax.numpy as jnp
from jax import lax
from jax.experimental import pallas as pl
from jax.experimental.pallas import tpu as pltpu
from jax.sharding import PartitionSpec as P

ROUND = 4
SIDE = 4
SHIFTS = (0, 1, 3, 2)
PARTS = 1
VMEM_LIMIT = 40 * 2**20
SMALL_LIMIT = 10 * 2**20


def split_kernel(slot_ref, source_ref, matrix_hbm, high_ref, low_ref, matrix_ref, sems, *, piece, first):
    count = matrix_ref.shape[0] // piece
    owners = matrix_ref.shape[1] // piece
    width = ROUND * piece
    rounds = [(i, j) for i in range(count // ROUND) for j in range(owners // ROUND)]
    arriving = {}
    for i, j in rounds:
        across = pl.ds(j * width, width)
        for n in range(i * ROUND, (i + 1) * ROUND):
            there = pl.ds(pl.multiple_of(source_ref[first + n] * piece, piece), piece)
            copy = pltpu.make_async_copy(
                matrix_hbm.at[there, across], matrix_ref.at[pl.ds(n * piece, piece), across], sems.at[n, j]
            )
            copy.start()
            arriving[n, j] = copy
    for i, j in rounds:
        for n in range(i * ROUND, (i + 1) * ROUND):
            arriving[n, j].wait()
        cols = slice(i * width, (i + 1) * width)
        turned = matrix_ref[cols, j * width : (j + 1) * width].T
        for k in range(ROUND):
            rows = turned[k * piece : (k + 1) * piece]
            high = rows.astype(jnp.bfloat16)
            at = pl.ds(pl.multiple_of(slot_ref[j * ROUND + k] * piece, piece), piece)
            high_ref[at, cols] = high
            low_ref[at, cols] = (rows - high.astype(jnp.float32)).astype(jnp.bfloat16)


def split_matrix(slots, sources, columns, piece, first, count):
    rows = columns.shape[1]
    depth = count * piece
    scalars = pl.BlockSpec(memory_space=pltpu.SMEM)
    on_chip = pl.BlockSpec(memory_space=pltpu.VMEM)
    out = pltpu.VMEM((rows, depth), jnp.bfloat16)
    return pl.pallas_call(
        functools.partial(split_kernel, piece=piece, first=first),
        in_specs=[scalars, scalars, pl.BlockSpec(memory_space=pltpu.HBM)],
        out_specs=[on_chip, on_chip],
        out_shape=[out, out],
        scratch_shapes=[pltpu.VMEM((depth, rows), jnp.float32), pltpu.SemaphoreType.DMA((count, rows // (ROUND * piece)))],
        compiler_params=pltpu.CompilerParams(vmem_limit_bytes=VMEM_LIMIT),
        name="split_matrix",
    )(slots, sources, pltpu.with_memory_space_constraint(columns, pltpu.HBM))


def product_kernel(*refs, half, parts):
    matrix, vectors, out_ref = refs[: 2 * parts], refs[2 * parts : -1], refs[-1]
    rows, width = out_ref.shape
    at = pl.ds(half * rows, rows)
    each = len(vectors) // parts
    total = None
    for n in range(parts):
        part = jnp.concatenate([v[...] for v in vectors[n * each : (n + 1) * each]], axis=0)
        top = part.astype(jnp.bfloat16)
        rest = (part - top.astype(jnp.float32)).astype(jnp.bfloat16)
        both = jnp.concatenate([top, rest], axis=1)
        main = jnp.dot(matrix[2 * n][at, :], both, preferred_element_type=jnp.float32)
        small = jnp.dot(matrix[2 * n + 1][at, :], top, preferred_element_type=jnp.float32)
        part_sum = main[:, :width] + (main[:, width:] + small)
        total = part_sum if total is None else total + part_sum
    out_ref[...] = total


def product(matrix, vectors, half):
    rows = matrix[0].shape[0] // 2
    on_chip = pl.BlockSpec(memory_space=pltpu.VMEM)
    return pl.pallas_call(
        functools.partial(product_kernel, half=half, parts=len(matrix) // 2),
        in_specs=[on_chip] * (len(matrix) + len(vectors)),
        out_specs=on_chip,
        out_shape=jax.ShapeDtypeStruct((rows, vectors[0].shape[1]), jnp.float32),
        compiler_params=pltpu.CompilerParams(vmem_limit_bytes=SMALL_LIMIT),
        name="product",
    )(*matrix, *vectors)


def gather_pairs(first, shift):
    pairs = []
    for y in range(SIDE):
        for x in range(SIDE):
            for core in range(2):
                along_x = (core == 0) == first
                to = (y, (x + shift) % SIDE) if along_x else ((y + shift) % SIDE, x)
                pairs.append(((y * SIDE + x) * 2 + core, (to[0] * SIDE + to[1]) * 2 + core))
    return pairs


def first_round(part):
    return [lax.ppermute(part, ("row", "depth"), gather_pairs(True, shift)) for shift in SHIFTS[1:]]


def second_round(line):
    return [line] + [lax.ppermute(line, ("row", "depth"), gather_pairs(False, shift)) for shift in SHIFTS[1:]]


def sources_here():
    row, core = lax.axis_index("row"), lax.axis_index("depth")
    row, core = row.astype(jnp.uint32), core.astype(jnp.int32)
    y, x = (row // SIDE).astype(jnp.int32), (row % SIDE).astype(jnp.int32)
    place = jnp.arange(SIDE * SIDE, dtype=jnp.int32)
    inner, outer = place % SIDE, place // SIDE
    inner, outer = inner ^ (inner >> 1), outer ^ (outer >> 1)
    y = (y - jnp.where(core == 0, outer, inner)) & (SIDE - 1)
    x = (x - jnp.where(core == 0, inner, outer)) & (SIDE - 1)
    return (y * SIDE + x).astype(jnp.int32)


def slots_here():
    ring = lax.axis_size("col")
    core, place = lax.axis_index("depth"), lax.axis_index("col")
    owner = jnp.arange(2 * ring, dtype=jnp.int32)
    chip, owner_core = owner // 2, owner % 2
    ahead = jnp.remainder(chip - place, ring)
    half = ring // 2
    before = ahead > half
    hops = jnp.where(before, ring - ahead, ahead)
    shared = (ahead == 0) | (ahead == half)
    handler = jnp.where(shared, owner_core, before.astype(jnp.int32))
    slot = jnp.where(shared, jnp.where(ahead == 0, ring - 1, ring - 2), 2 * (hops - 1) + owner_core)
    return (jnp.where(handler == core, 0, ring) + slot).astype(jnp.int32)


SWAP = [(0, 1), (1, 0)]


def to_owners(ours, theirs, core_row, piece):
    width = ours.shape[-1]
    ring = lax.axis_size("col")
    received = lax.ppermute(theirs, "depth", SWAP)
    summed = (ours + received).reshape(-1, piece, width)
    axes = ("col", "depth")

    def pairs(hops):
        return [(2 * z + c, 2 * ((z + (1 - 2 * c) * hops) % ring) + c) for z in range(ring) for c in range(2)]

    half = ring // 2
    arrived = []
    for hops in range(1, half):
        arrived.append(lax.ppermute(summed[2 * (hops - 1) : 2 * hops], axes, pairs(hops)))
    opposite = lax.ppermute(summed[ring - 2], axes, pairs(half))
    both = sum(arrived[1:], arrived[0])
    first_core = core_row == 0
    give = jnp.where(first_core, both[1], both[0])
    keep = jnp.where(first_core, both[0], both[1])
    last = lax.ppermute(give, "depth", SWAP)
    return summed[ring - 1] + opposite + keep + last


def body(matrix_columns, sources):
    rows_here = matrix_columns.shape[3]
    piece, width = sources.shape[2:]
    columns = matrix_columns.reshape(-1, rows_here)
    core_row = jnp.broadcast_to(lax.axis_index("depth"), (1, width))
    slots, order, core_row = lax.optimization_barrier((slots_here(), sources_here(), core_row))
    part = sources.reshape(piece, width)
    others = first_round(part)
    count = columns.shape[0] // piece // PARTS
    matrix = []
    results = []
    for step in range(2):
        gathered = second_round(jnp.concatenate([part] + list(others), axis=0))
        for n in range(len(matrix) // 2, PARTS):
            matrix = matrix + list(split_matrix(slots, order, columns, piece, n * count, count))
        theirs = product(matrix, gathered, 1)
        ours = product(matrix, gathered, 0)
        part = to_owners(ours, theirs, core_row, piece)
        results.append(part)
        if step == 0:
            others = first_round(part)
    return tuple(r.reshape(sources.shape) for r in results)


def solution(mesh):
    in_specs = (P(None, ("col", "depth"), None, "row"), P("row", ("col", "depth"), None, None))
    out_specs = (P("row", ("col", "depth"), None, None), P("row", ("col", "depth"), None, None))
    return jax.shard_map(body, mesh=mesh, in_specs=in_specs, out_specs=out_specs, check_vma=False)
```

time: 120 us -> 81.9 us (0.68)
  blocking collectives: 77.4 us -> 0 us
  starting transfers between devices: 7.58 us -> 44.2 us
  waiting for transfers between devices: 3.54 us -> 23.2 us
  matrix products: 18.3 us -> 0 us
  Pallas kernels: 0 us -> 11.8 us
  local copies, waits for them, and re-layouts: 11.7 us -> 0.06 us
    all_to_all x3 -> x0, blocking collectives: 77.4 us -> none  [the longest x2 59.5 us: sent_and_summed(): tiles = lax.all_to_all(cut_along(shard, dim, peers), axis, 0, 0, tiled=True)]
    ppermute x0 -> x24, starting transfers between devices: none -> 44.2 us  [the longest x6 11.3 us: to_owners(): lax.ppermute(summed[2 * (hops - 1):2 * hops], axes, pairs(hops))]
    ppermute x0 -> x24, waiting for transfers between devices: none -> 23.2 us  [the longest x6 7.82 us: first_round(): lax.ppermute(part, ('row', 'depth'), gather_pairs(True, shift))]
    dot_general x2 -> x0, matrix products: 18.3 us -> none  [contract(): lax.dot_general(window, inputs_flat, (((0,), (0,)), ((), ())), precision=...]
    pallas_call x0 -> x5, Pallas kernels: none -> 11.8 us  [the longest x1 6.31 us: split_matrix(): pl.pallas_call(functools.partial(split_kernel, piece=piece, first=first),...]
    dot_general x2 -> x0, local copies, waits for them, and re-layouts: 9.9 us -> none  [contract(): lax.dot_general(window, inputs_flat, (((0,), (0,)), ((), ())), precision=...]
    all_to_all x1 -> x0, starting transfers between devices: 7.58 us -> none  [copy_for_each(): return lax.all_to_all(copies, axis, split_axis=0, concat_axis=0, tiled=True)]
    all_to_all x1 -> x0, waiting for transfers between devices: 3.54 us -> none  [copy_for_each(): return lax.all_to_all(copies, axis, split_axis=0, concat_axis=0, tiled=True)]
  transfers between devices with their start and end apart: 1 -> 24, of which waited for: 1 -> 14; matrix products, arithmetic and copies ran while one was open for 8% -> 0% of each run, Pallas kernels for 0% -> 11%
where the time goes in v2:
time: 81.9 us; the launch traced here: 81.7 us
  starting transfers between devices  44.2 us (54%)
  waiting for transfers between devices  23.2 us (28%)
  Pallas kernels  11.8 us (14%)
  other arithmetic  1.65 us (2%)
    ppermute x6, starting transfers between devices, to_owners(): lax.ppermute(summed[2 * (hops - 1):2 * hops], axes, pairs(hops))  11.3 us
    ppermute x2, starting transfers between devices, to_owners(): opposite = lax.ppermute(summed[ring - 2], axes, pairs(half))  8.21 us
    ppermute x6, starting transfers between devices, first_round(): lax.ppermute(part, ('row', 'depth'), gather_pairs(True, shift))  8.18 us
    ppermute x6, waiting for transfers between devices, first_round(): lax.ppermute(part, ('row', 'depth'), gather_pairs(True, shift))  7.82 us
    ppermute x6, waiting for transfers between devices, to_owners(): lax.ppermute(summed[2 * (hops - 1):2 * hops], axes, pairs(hops))  7.02 us
    ppermute x2, starting transfers between devices, to_owners(): received = lax.ppermute(theirs, 'depth', SWAP)  6.94 us
    ppermute x6, waiting for transfers between devices, second_round(): lax.ppermute(line, ('row', 'depth'), gather_pairs(False, shift))  6.6 us
    pallas_call x1, Pallas kernels, split_matrix(): pl.pallas_call(functools.partial(split_kernel, piece=piece, first=first),...  6.31 us
  transfers between devices with their start and end apart: 24, of which 14 were waited for; matrix products, arithmetic and copies ran while one was open for 0% of the time, Pallas kernels for 11%

profile of v2, /device:TPU:1, one launch (start us, length us, event | category | flops | bytes accessed | tf_op | source)
XLA Modules:
  0.0 81.7 jit_solution(16779546397918386951)
XLA Ops:
  0.6 3.8 %collective-permute-start.2 = (f32[96,128]{1,0:T(8,128)}, f32[96,128]{1,0:T(8,128)S(1)}, u32[]{:S(2)}, u32[]{:S(2)}) collective-permute-start(f32[96,128]{1,0:T(8,128)} %bitcast.45), channel_id=1, source_target_pairs={{0,32},{1,129},{16,48},{17,145},{32,0},{33,161},{48,16},{49,177},{... | collective-permute-start | bytes 147464 | tf_op jit(solution)/shard_map/ppermute | solution.py:106
  4.5 0.8 collective-permute-start.1
  5.2 0.7 collective-permute-start
  5.9 0.2 collective-permute-done.2
  6.2 1.5 %collective-permute-done.1 = f32[96,128]{1,0:T(8,128)S(1)} collective-permute-done((f32[96,128]{1,0:T(8,128)}, f32[96,128]{1,0:T(8,128)S(1)}, u32[]{:S(2)}, u32[]{:S(2)}) %collective-permute-start.1) | collective-permute-done | bytes 49184 | tf_op jit(solution)/shard_map/ppermute | solution.py:106
  7.6 2.0 %collective-permute-done = f32[96,128]{1,0:T(8,128)S(1)} collective-permute-done((f32[96,128]{1,0:T(8,128)}, f32[96,128]{1,0:T(8,128)S(1)}, u32[]{:S(2)}, u32[]{:S(2)}) %collective-permute-start) | collective-permute-done | bytes 49184 | tf_op jit(solution)/shard_map/ppermute | solution.py:106
  9.6 0.8 pad_maximum_fusion.refs_2_
  10.4 2.8 %collective-permute-start.5 = (f32[384,128]{1,0:T(8,128)S(1)}, f32[384,128]{1,0:T(8,128)S(1)}, u32[]{:S(2)}, u32[]{:S(2)}) collective-permute-start(f32[384,128]{1,0:T(8,128)S(1)} %pad_maximum_fusion.refs_2_), channel_id=1, source_target_pairs={{0,128},{1,33},{16,144},{17,49},{32,160},{33,1},{48,176},{49,17},{... | collective-permute-start | bytes 589832 | tf_op jit(solution)/shard_map/ppermute | solution.py:110
  13.2 0.9 %collective-permute-start.4 = (f32[384,128]{1,0:T(8,128)S(1)}, f32[384,128]{1,0:T(8,128)S(1)}, u32[]{:S(2)}, u32[]{:S(2)}) collective-permute-start(f32[384,128]{1,0:T(8,128)S(1)} %pad_maximum_fusion.refs_2_), channel_id=1, source_target_pairs={{0,192},{1,49},{16,208},{17,1},{32,224},{33,17},{48,240},{49,33},{... | collective-permute-start | bytes 589832 | tf_op jit(solution)/shard_map/ppermute | solution.py:110
  14.1 0.6 collective-permute-start.3
  14.7 6.3 %split_matrix.1 = (bf16[1536,1536]{1,0:T(8,128)(2,1)S(1)}, bf16[1536,1536]{1,0:T(8,128)(2,1)S(1)}) custom-call(s32[16]{0:T(128)S(1)} %get-tuple-element.7.slot_ref, s32[16]{0:T(128)S(1)} %get-tuple-element.8.source_ref, f32[1536,1536]{1,0:T(8,128)} %bitcast.37), custom_call_target="tpu_custom_call" | custom-call | tf_op jit(solution)/shard_map/split_matrix/pallas_call | solution.py:52
  21.1 0.0 collective-permute-done.5.refs_5_
  21.1 0.0 collective-permute-done.4.refs_4_
  21.1 0.0 collective-permute-done.3.refs_3_
  21.1 1.4 %product.5 = f32[768,128]{1,0:T(8,128)S(1)} custom-call(bf16[1536,1536]{1,0:T(8,128)(2,1)S(1)} %get-tuple-element.9.refs_0_, bf16[1536,1536]{1,0:T(8,128)(2,1)S(1)} %get-tuple-element.10.refs_1_, f32[384,128]{1,0:T(8,128)S(1)} %pad_maximum_fusion.refs_2_, f32[384,128]{1,0:T(8,128)S(1)} %collective-permute-done.3.refs_3_, ...), custom_call_target="tpu_custom_call" | custom-call | tf_op jit(solution)/shard_map/product/pallas_call | solution.py:84
  22.5 3.4 %collective-permute-start.6 = (f32[768,128]{1,0:T(8,128)S(1)}, f32[768,128]{1,0:T(8,128)S(1)}, u32[]{:S(2)}, u32[]{:S(2)}) collective-permute-start(f32[768,128]{1,0:T(8,128)S(1)} %product.5), channel_id=1, source_target_pairs={{0,1},{1,0},{2,3},{3,2},{4,5},{5,4},{6,7},{7,6},{8,9},{9,8},{10,11... | collective-permute-start | bytes 1179656 | tf_op jit(solution)/shard_map/ppermute | solution.py:146
  25.9 1.4 %product.4 = f32[768,128]{1,0:T(8,128)S(1)} custom-call(bf16[1536,1536]{1,0:T(8,128)(2,1)S(1)} %get-tuple-element.9.refs_0_, bf16[1536,1536]{1,0:T(8,128)(2,1)S(1)} %get-tuple-element.10.refs_1_, f32[384,128]{1,0:T(8,128)S(1)} %pad_maximum_fusion.refs_2_, f32[384,128]{1,0:T(8,128)S(1)} %collective-permute-done.3.refs_3_, ...), custom_call_target="tpu_custom_call" | custom-call | tf_op jit(solution)/shard_map/product/pallas_call | solution.py:84
  27.3 0.0 collective-permute-done.6
  27.3 0.1 add.74
  27.4 6.5 %collective-permute-start.10 = (f32[2,96,128]{2,1,0:T(8,128)S(1)}, f32[2,96,128]{2,1,0:T(8,128)S(1)}, u32[]{:S(2)}, u32[]{:S(2)}) collective-permute-start(f32[2,96,128]{2,1,0:T(8,128)S(1)} %bitcast.43), channel_id=1, source_target_pairs={{0,6},{1,11},{2,8},{3,13},{4,10},{5,15},{6,12},{7,1},{8,14},{9,3},... | collective-permute-start | bytes 294920 | tf_op jit(solution)/shard_map/ppermute | solution.py:156
  33.9 0.3 collective-permute-start.9
  34.2 0.5 collective-permute-start.8
  34.6 4.6 %collective-permute-start.7 = (f32[96,128]{1,0:T(8,128)S(1)}, f32[96,128]{1,0:T(8,128)S(1)}, u32[]{:S(2)}, u32[]{:S(2)}) collective-permute-start(f32[96,128]{1,0:T(8,128)S(1)} %slice.89), channel_id=1, source_target_pairs={{0,8},{1,9},{2,10},{3,11},{4,12},{5,13},{6,14},{7,15},{8,0},{9,1},... | collective-permute-start | bytes 147464 | tf_op jit(solution)/shard_map/ppermute | solution.py:157
  39.2 0.0 collective-permute-done.10
  39.2 0.9 %collective-permute-done.9 = f32[2,96,128]{2,1,0:T(8,128)S(1)} collective-permute-done((f32[2,96,128]{2,1,0:T(8,128)S(1)}, f32[2,96,128]{2,1,0:T(8,128)S(1)}, u32[]{:S(2)}, u32[]{:S(2)}) %collective-permute-start.9) | collective-permute-done | bytes 98336 | tf_op jit(solution)/shard_map/ppermute | solution.py:156
  40.1 2.2 %collective-permute-done.8 = f32[2,96,128]{2,1,0:T(8,128)S(1)} collective-permute-done((f32[2,96,128]{2,1,0:T(8,128)S(1)}, f32[2,96,128]{2,1,0:T(8,128)S(1)}, u32[]{:S(2)}, u32[]{:S(2)}) %collective-permute-start.8) | collective-permute-done | bytes 98336 | tf_op jit(solution)/shard_map/ppermute | solution.py:156
  42.3 2.2 %collective-permute-start.11 = (f32[96,128]{1,0:T(8,128)S(1)}, f32[96,128]{1,0:T(8,128)S(1)}, u32[]{:S(2)}, u32[]{:S(2)}) collective-permute-start(f32[96,128]{1,0:T(8,128)S(1)} %fusion.5), channel_id=1, source_target_pairs={{0,1},{1,0},{2,3},{3,2},{4,5},{5,4},{6,7},{7,6},{8,9},{9,8},{10,11... | collective-permute-start | bytes 147464 | tf_op jit(solution)/shard_map/ppermute | solution.py:162
  44.6 0.0 collective-permute-done.7
  44.6 0.9 %collective-permute-done.11 = f32[96,128]{1,0:T(8,128)S(1)} collective-permute-done((f32[96,128]{1,0:T(8,128)S(1)}, f32[96,128]{1,0:T(8,128)S(1)}, u32[]{:S(2)}, u32[]{:S(2)}) %collective-permute-start.11) | collective-permute-done | bytes 49184 | tf_op jit(solution)/shard_map/ppermute | solution.py:162
  45.5 0.0 copy-start
  45.5 0.7 collective-permute-start.14
  46.2 2.2 %collective-permute-start.13 = (f32[96,128]{1,0:T(8,128)S(1)}, f32[96,128]{1,0:T(8,128)S(1)}, u32[]{:S(2)}, u32[]{:S(2)}) collective-permute-start(f32[96,128]{1,0:T(8,128)S(1)} %fusion.4), channel_id=1, source_target_pairs={{0,48},{1,193},{16,0},{17,209},{32,16},{33,225},{48,32},{49,241},{... | collective-permute-start | bytes 147464 | tf_op jit(solution)/shard_map/ppermute | solution.py:106
  48.4 0.0 collective-permute-start.12
  48.4 1.6 %collective-permute-done.14 = f32[96,128]{1,0:T(8,128)S(1)} collective-permute-done((f32[96,128]{1,0:T(8,128)S(1)}, f32[96,128]{1,0:T(8,128)S(1)}, u32[]{:S(2)}, u32[]{:S(2)}) %collective-permute-start.14) | collective-permute-done | bytes 49184 | tf_op jit(solution)/shard_map/ppermute | solution.py:106
  50.0 0.4 collective-permute-done.13
  50.4 2.1 %collective-permute-done.12 = f32[96,128]{1,0:T(8,128)S(1)} collective-permute-done((f32[96,128]{1,0:T(8,128)S(1)}, f32[96,128]{1,0:T(8,128)S(1)}, u32[]{:S(2)}, u32[]{:S(2)}) %collective-permute-start.12) | collective-permute-done | bytes 49184 | tf_op jit(solution)/shard_map/ppermute | solution.py:106
  52.5 0.1 collective-permute-start.17
  52.7 1.8 %collective-permute-start.16 = (f32[384,128]{1,0:T(8,128)S(1)}, f32[384,128]{1,0:T(8,128)S(1)}, u32[]{:S(2)}, u32[]{:S(2)}) collective-permute-start(f32[384,128]{1,0:T(8,128)S(1)} %pad_maximum_fusion.1.refs_2_), channel_id=1, source_target_pairs={{0,192},{1,49},{16,208},{17,1},{32,224},{33,17},{48,240},{49,33},{... | collective-permute-start | bytes 589832 | tf_op jit(solution)/shard_map/ppermute | solution.py:110
  54.4 0.0 collective-permute-start.15
  54.4 4.5 %collective-permute-done.17.refs_5_ = f32[384,128]{1,0:T(8,128)S(1)} collective-permute-done((f32[384,128]{1,0:T(8,128)S(1)}, f32[384,128]{1,0:T(8,128)S(1)}, u32[]{:S(2)}, u32[]{:S(2)}) %collective-permute-start.17) | collective-permute-done | bytes 196640 | tf_op jit(solution)/shard_map/ppermute | solution.py:110
  59.0 0.0 collective-permute-done.16.refs_4_
  59.0 2.1 %collective-permute-done.15.refs_3_ = f32[384,128]{1,0:T(8,128)S(1)} collective-permute-done((f32[384,128]{1,0:T(8,128)S(1)}, f32[384,128]{1,0:T(8,128)S(1)}, u32[]{:S(2)}, u32[]{:S(2)}) %collective-permute-start.15) | collective-permute-done | bytes 196640 | tf_op jit(solution)/shard_map/ppermute | solution.py:110
  61.0 1.4 %product.7 = f32[768,128]{1,0:T(8,128)S(1)} custom-call(bf16[1536,1536]{1,0:T(8,128)(2,1)S(1)} %get-tuple-element.9.refs_0_, bf16[1536,1536]{1,0:T(8,128)(2,1)S(1)} %get-tuple-element.10.refs_1_, f32[384,128]{1,0:T(8,128)S(1)} %pad_maximum_fusion.1.refs_2_, f32[384,128]{1,0:T(8,128)S(1)} %collective-permute-done.15.refs_3_, ...), custom_call_target="tpu_custom_call" | custom-call | tf_op jit(solution)/shard_map/product/pallas_call | solution.py:84
  62.4 0.0 copy-done
  62.4 3.5 %collective-permute-start.18 = (f32[768,128]{1,0:T(8,128)S(1)}, f32[768,128]{1,0:T(8,128)S(1)}, u32[]{:S(2)}, u32[]{:S(2)}) collective-permute-start(f32[768,128]{1,0:T(8,128)S(1)} %product.7), channel_id=1, source_target_pairs={{0,1},{1,0},{2,3},{3,2},{4,5},{5,4},{6,7},{7,6},{8,9},{9,8},{10,11... | collective-permute-start | bytes 1179656 | tf_op jit(solution)/shard_map/ppermute | solution.py:146
  66.0 1.4 %product.6 = f32[768,128]{1,0:T(8,128)S(1)} custom-call(bf16[1536,1536]{1,0:T(8,128)(2,1)S(1)} %get-tuple-element.9.refs_0_, bf16[1536,1536]{1,0:T(8,128)(2,1)S(1)} %get-tuple-element.10.refs_1_, f32[384,128]{1,0:T(8,128)S(1)} %pad_maximum_fusion.1.refs_2_, f32[384,128]{1,0:T(8,128)S(1)} %collective-permute-done.15.refs_3_, ...), custom_call_target="tpu_custom_call" | custom-call | tf_op jit(solution)/shard_map/product/pallas_call | solution.py:84
  67.3 0.0 collective-permute-done.18
  67.4 1.4 %collective-permute-start.22 = (f32[2,96,128]{2,1,0:T(8,128)S(1)}, f32[2,96,128]{2,1,0:T(8,128)S(1)}, u32[]{:S(2)}, u32[]{:S(2)}) collective-permute-start(f32[2,96,128]{2,1,0:T(8,128)S(1)} %bitcast.44), channel_id=1, source_target_pairs={{0,6},{1,11},{2,8},{3,13},{4,10},{5,15},{6,12},{7,1},{8,14},{9,3},... | collective-permute-start | bytes 294920 | tf_op jit(solution)/shard_map/ppermute | solution.py:156
  68.9 1.8 %collective-permute-start.21 = (f32[2,96,128]{2,1,0:T(8,128)S(1)}, f32[2,96,128]{2,1,0:T(8,128)S(1)}, u32[]{:S(2)}, u32[]{:S(2)}) collective-permute-start(f32[2,96,128]{2,1,0:T(8,128)S(1)} %bitcast.42), channel_id=1, source_target_pairs={{0,4},{1,13},{2,6},{3,15},{4,8},{5,1},{6,10},{7,3},{8,12},{9,5},{1... | collective-permute-start | bytes 294920 | tf_op jit(solution)/shard_map/ppermute | solution.py:156
  70.6 0.9 %collective-permute-start.20 = (f32[2,96,128]{2,1,0:T(8,128)S(1)}, f32[2,96,128]{2,1,0:T(8,128)S(1)}, u32[]{:S(2)}, u32[]{:S(2)}) collective-permute-start(f32[2,96,128]{2,1,0:T(8,128)S(1)} %bitcast.40), channel_id=1, source_target_pairs={{0,2},{1,15},{2,4},{3,1},{4,6},{5,3},{6,8},{7,5},{8,10},{9,7},{10,... | collective-permute-start | bytes 294920 | tf_op jit(solution)/shard_map/ppermute | solution.py:156
  71.5 3.6 %collective-permute-start.19 = (f32[96,128]{1,0:T(8,128)S(1)}, f32[96,128]{1,0:T(8,128)S(1)}, u32[]{:S(2)}, u32[]{:S(2)}) collective-permute-start(f32[96,128]{1,0:T(8,128)S(1)} %slice.96), channel_id=1, source_target_pairs={{0,8},{1,9},{2,10},{3,11},{4,12},{5,13},{6,14},{7,15},{8,0},{9,1},... | collective-permute-start | bytes 147464 | tf_op jit(solution)/shard_map/ppermute | solution.py:157
  75.2 0.0 collective-permute-done.22
  75.2 1.7 %collective-permute-done.21 = f32[2,96,128]{2,1,0:T(8,128)S(1)} collective-permute-done((f32[2,96,128]{2,1,0:T(8,128)S(1)}, f32[2,96,128]{2,1,0:T(8,128)S(1)}, u32[]{:S(2)}, u32[]{:S(2)}) %collective-permute-start.21) | collective-permute-done | bytes 98336 | tf_op jit(solution)/shard_map/ppermute | solution.py:156
  76.9 2.2 %collective-permute-done.20 = f32[2,96,128]{2,1,0:T(8,128)S(1)} collective-permute-done((f32[2,96,128]{2,1,0:T(8,128)S(1)}, f32[2,96,128]{2,1,0:T(8,128)S(1)}, u32[]{:S(2)}, u32[]{:S(2)}) %collective-permute-start.20) | collective-permute-done | bytes 98336 | tf_op jit(solution)/shard_map/ppermute | solution.py:156
  79.1 1.1 %collective-permute-start.23 = (f32[96,128]{1,0:T(8,128)S(1)}, f32[96,128]{1,0:T(8,128)S(1)}, u32[]{:S(2)}, u32[]{:S(2)}) collective-permute-start(f32[96,128]{1,0:T(8,128)S(1)} %fusion.6), channel_id=1, source_target_pairs={{0,1},{1,0},{2,3},{3,2},{4,5},{5,4},{6,7},{7,6},{8,9},{9,8},{10,11... | collective-permute-start | bytes 147464 | tf_op jit(solution)/shard_map/ppermute | solution.py:162
  80.2 0.0 collective-permute-done.19
  80.2 0.9 %collective-permute-done.23 = f32[96,128]{1,0:T(8,128)S(1)} collective-permute-done((f32[96,128]{1,0:T(8,128)S(1)}, f32[96,128]{1,0:T(8,128)S(1)}, u32[]{:S(2)}, u32[]{:S(2)}) %collective-permute-start.23) | collective-permute-done | bytes 49184 | tf_op jit(solution)/shard_map/ppermute | solution.py:162
  81.1 0.6 fusion.2
  (14 shorter events, 0.2 us)
Async XLA Ops:
  0.6 5.5 %collective-permute-start.2 = (f32[96,128]{1,0:T(8,128)}, f32[96,128]{1,0:T(8,128)S(1)}, u32[]{:S(2)}, u32[]{:S(2)}) collective-permute-start(f32[96,128]{1,0:T(8,128)} %bitcast.45), channel_id=1, source_target_pairs={{0,32},{1,129},{16,48},{17,145},{32,0},{33,161},{48,16},{49,177},{... | collective-permute-start | bytes 147464 | tf_op jit(solution)/shard_map/ppermute | solution.py:106
  4.5 3.2 %collective-permute-start.1 = (f32[96,128]{1,0:T(8,128)}, f32[96,128]{1,0:T(8,128)S(1)}, u32[]{:S(2)}, u32[]{:S(2)}) collective-permute-start(f32[96,128]{1,0:T(8,128)} %bitcast.46), channel_id=1, source_target_pairs={{0,48},{1,193},{16,0},{17,209},{32,16},{33,225},{48,32},{49,241},{... | collective-permute-start | bytes 147464 | tf_op jit(solution)/shard_map/ppermute | solution.py:106
  5.2 4.4 %collective-permute-start = (f32[96,128]{1,0:T(8,128)}, f32[96,128]{1,0:T(8,128)S(1)}, u32[]{:S(2)}, u32[]{:S(2)}) collective-permute-start(f32[96,128]{1,0:T(8,128)} %bitcast.47), channel_id=1, source_target_pairs={{0,16},{1,65},{16,32},{17,81},{32,48},{33,97},{48,0},{49,113},{64,... | collective-permute-start | bytes 147464 | tf_op jit(solution)/shard_map/ppermute | solution.py:106
  10.4 10.6 %collective-permute-start.5 = (f32[384,128]{1,0:T(8,128)S(1)}, f32[384,128]{1,0:T(8,128)S(1)}, u32[]{:S(2)}, u32[]{:S(2)}) collective-permute-start(f32[384,128]{1,0:T(8,128)S(1)} %pad_maximum_fusion.refs_2_), channel_id=1, source_target_pairs={{0,128},{1,33},{16,144},{17,49},{32,160},{33,1},{48,176},{49,17},{... | collective-permute-start | bytes 589832 | tf_op jit(solution)/shard_map/ppermute | solution.py:110
  13.2 7.8 %collective-permute-start.4 = (f32[384,128]{1,0:T(8,128)S(1)}, f32[384,128]{1,0:T(8,128)S(1)}, u32[]{:S(2)}, u32[]{:S(2)}) collective-permute-start(f32[384,128]{1,0:T(8,128)S(1)} %pad_maximum_fusion.refs_2_), channel_id=1, source_target_pairs={{0,192},{1,49},{16,208},{17,1},{32,224},{33,17},{48,240},{49,33},{... | collective-permute-start | bytes 589832 | tf_op jit(solution)/shard_map/ppermute | solution.py:110
  14.1 7.0 %collective-permute-start.3 = (f32[384,128]{1,0:T(8,128)S(1)}, f32[384,128]{1,0:T(8,128)S(1)}, u32[]{:S(2)}, u32[]{:S(2)}) collective-permute-start(f32[384,128]{1,0:T(8,128)S(1)} %pad_maximum_fusion.refs_2_), channel_id=1, source_target_pairs={{0,64},{1,17},{16,80},{17,33},{32,96},{33,49},{48,112},{49,1},{64,... | collective-permute-start | bytes 589832 | tf_op jit(solution)/shard_map/ppermute | solution.py:110
  22.5 4.8 %collective-permute-start.6 = (f32[768,128]{1,0:T(8,128)S(1)}, f32[768,128]{1,0:T(8,128)S(1)}, u32[]{:S(2)}, u32[]{:S(2)}) collective-permute-start(f32[768,128]{1,0:T(8,128)S(1)} %product.5), channel_id=1, source_target_pairs={{0,1},{1,0},{2,3},{3,2},{4,5},{5,4},{6,7},{7,6},{8,9},{9,8},{10,11... | collective-permute-start | bytes 1179656 | tf_op jit(solution)/shard_map/ppermute | solution.py:146
  27.4 11.9 %collective-permute-start.10 = (f32[2,96,128]{2,1,0:T(8,128)S(1)}, f32[2,96,128]{2,1,0:T(8,128)S(1)}, u32[]{:S(2)}, u32[]{:S(2)}) collective-permute-start(f32[2,96,128]{2,1,0:T(8,128)S(1)} %bitcast.43), channel_id=1, source_target_pairs={{0,6},{1,11},{2,8},{3,13},{4,10},{5,15},{6,12},{7,1},{8,14},{9,3},... | collective-permute-start | bytes 294920 | tf_op jit(solution)/shard_map/ppermute | solution.py:156
  33.9 6.2 %collective-permute-start.9 = (f32[2,96,128]{2,1,0:T(8,128)S(1)}, f32[2,96,128]{2,1,0:T(8,128)S(1)}, u32[]{:S(2)}, u32[]{:S(2)}) collective-permute-start(f32[2,96,128]{2,1,0:T(8,128)S(1)} %bitcast.41), channel_id=1, source_target_pairs={{0,4},{1,13},{2,6},{3,15},{4,8},{5,1},{6,10},{7,3},{8,12},{9,5},{1... | collective-permute-start | bytes 294920 | tf_op jit(solution)/shard_map/ppermute | solution.py:156
  34.2 8.1 %collective-permute-start.8 = (f32[2,96,128]{2,1,0:T(8,128)S(1)}, f32[2,96,128]{2,1,0:T(8,128)S(1)}, u32[]{:S(2)}, u32[]{:S(2)}) collective-permute-start(f32[2,96,128]{2,1,0:T(8,128)S(1)} %bitcast.39), channel_id=1, source_target_pairs={{0,2},{1,15},{2,4},{3,1},{4,6},{5,3},{6,8},{7,5},{8,10},{9,7},{10,... | collective-permute-start | bytes 294920 | tf_op jit(solution)/shard_map/ppermute | solution.py:156
  34.6 9.9 %collective-permute-start.7 = (f32[96,128]{1,0:T(8,128)S(1)}, f32[96,128]{1,0:T(8,128)S(1)}, u32[]{:S(2)}, u32[]{:S(2)}) collective-permute-start(f32[96,128]{1,0:T(8,128)S(1)} %slice.89), channel_id=1, source_target_pairs={{0,8},{1,9},{2,10},{3,11},{4,12},{5,13},{6,14},{7,15},{8,0},{9,1},... | collective-permute-start | bytes 147464 | tf_op jit(solution)/shard_map/ppermute | solution.py:157
  42.3 3.1 %collective-permute-start.11 = (f32[96,128]{1,0:T(8,128)S(1)}, f32[96,128]{1,0:T(8,128)S(1)}, u32[]{:S(2)}, u32[]{:S(2)}) collective-permute-start(f32[96,128]{1,0:T(8,128)S(1)} %fusion.5), channel_id=1, source_target_pairs={{0,1},{1,0},{2,3},{3,2},{4,5},{5,4},{6,7},{7,6},{8,9},{9,8},{10,11... | collective-permute-start | bytes 147464 | tf_op jit(solution)/shard_map/ppermute | solution.py:162
  45.5 16.9 %copy-start = (f32[96,128]{1,0:T(8,128)}, f32[96,128]{1,0:T(8,128)S(1)}, u32[]{:S(2)}) copy-start(f32[96,128]{1,0:T(8,128)S(1)} %fusion.4) | copy-start | bytes 147460
  45.5 4.5 %collective-permute-start.14 = (f32[96,128]{1,0:T(8,128)S(1)}, f32[96,128]{1,0:T(8,128)S(1)}, u32[]{:S(2)}, u32[]{:S(2)}) collective-permute-start(f32[96,128]{1,0:T(8,128)S(1)} %fusion.4), channel_id=1, source_target_pairs={{0,32},{1,129},{16,48},{17,145},{32,0},{33,161},{48,16},{49,177},{... | collective-permute-start | bytes 147464 | tf_op jit(solution)/shard_map/ppermute | solution.py:106
  46.2 4.3 %collective-permute-start.13 = (f32[96,128]{1,0:T(8,128)S(1)}, f32[96,128]{1,0:T(8,128)S(1)}, u32[]{:S(2)}, u32[]{:S(2)}) collective-permute-start(f32[96,128]{1,0:T(8,128)S(1)} %fusion.4), channel_id=1, source_target_pairs={{0,48},{1,193},{16,0},{17,209},{32,16},{33,225},{48,32},{49,241},{... | collective-permute-start | bytes 147464 | tf_op jit(solution)/shard_map/ppermute | solution.py:106
  48.4 4.2 %collective-permute-start.12 = (f32[96,128]{1,0:T(8,128)S(1)}, f32[96,128]{1,0:T(8,128)S(1)}, u32[]{:S(2)}, u32[]{:S(2)}) collective-permute-start(f32[96,128]{1,0:T(8,128)S(1)} %fusion.4), channel_id=1, source_target_pairs={{0,16},{1,65},{16,32},{17,81},{32,48},{33,97},{48,0},{49,113},{64,... | collective-permute-start | bytes 147464 | tf_op jit(solution)/shard_map/ppermute | solution.py:106
  52.5 6.4 %collective-permute-start.17 = (f32[384,128]{1,0:T(8,128)S(1)}, f32[384,128]{1,0:T(8,128)S(1)}, u32[]{:S(2)}, u32[]{:S(2)}) collective-permute-start(f32[384,128]{1,0:T(8,128)S(1)} %pad_maximum_fusion.1.refs_2_), channel_id=1, source_target_pairs={{0,128},{1,33},{16,144},{17,49},{32,160},{33,1},{48,176},{49,17},{... | collective-permute-start | bytes 589832 | tf_op jit(solution)/shard_map/ppermute | solution.py:110
  52.7 6.3 %collective-permute-start.16 = (f32[384,128]{1,0:T(8,128)S(1)}, f32[384,128]{1,0:T(8,128)S(1)}, u32[]{:S(2)}, u32[]{:S(2)}) collective-permute-start(f32[384,128]{1,0:T(8,128)S(1)} %pad_maximum_fusion.1.refs_2_), channel_id=1, source_target_pairs={{0,192},{1,49},{16,208},{17,1},{32,224},{33,17},{48,240},{49,33},{... | collective-permute-start | bytes 589832 | tf_op jit(solution)/shard_map/ppermute | solution.py:110
  54.4 6.6 %collective-permute-start.15 = (f32[384,128]{1,0:T(8,128)S(1)}, f32[384,128]{1,0:T(8,128)S(1)}, u32[]{:S(2)}, u32[]{:S(2)}) collective-permute-start(f32[384,128]{1,0:T(8,128)S(1)} %pad_maximum_fusion.1.refs_2_), channel_id=1, source_target_pairs={{0,64},{1,17},{16,80},{17,33},{32,96},{33,49},{48,112},{49,1},{64,... | collective-permute-start | bytes 589832 | tf_op jit(solution)/shard_map/ppermute | solution.py:110
  62.4 4.9 %collective-permute-start.18 = (f32[768,128]{1,0:T(8,128)S(1)}, f32[768,128]{1,0:T(8,128)S(1)}, u32[]{:S(2)}, u32[]{:S(2)}) collective-permute-start(f32[768,128]{1,0:T(8,128)S(1)} %product.7), channel_id=1, source_target_pairs={{0,1},{1,0},{2,3},{3,2},{4,5},{5,4},{6,7},{7,6},{8,9},{9,8},{10,11... | collective-permute-start | bytes 1179656 | tf_op jit(solution)/shard_map/ppermute | solution.py:146
  67.4 7.7 %collective-permute-start.22 = (f32[2,96,128]{2,1,0:T(8,128)S(1)}, f32[2,96,128]{2,1,0:T(8,128)S(1)}, u32[]{:S(2)}, u32[]{:S(2)}) collective-permute-start(f32[2,96,128]{2,1,0:T(8,128)S(1)} %bitcast.44), channel_id=1, source_target_pairs={{0,6},{1,11},{2,8},{3,13},{4,10},{5,15},{6,12},{7,1},{8,14},{9,3},... | collective-permute-start | bytes 294920 | tf_op jit(solution)/shard_map/ppermute | solution.py:156
  68.9 8.0 %collective-permute-start.21 = (f32[2,96,128]{2,1,0:T(8,128)S(1)}, f32[2,96,128]{2,1,0:T(8,128)S(1)}, u32[]{:S(2)}, u32[]{:S(2)}) collective-permute-start(f32[2,96,128]{2,1,0:T(8,128)S(1)} %bitcast.42), channel_id=1, source_target_pairs={{0,4},{1,13},{2,6},{3,15},{4,8},{5,1},{6,10},{7,3},{8,12},{9,5},{1... | collective-permute-start | bytes 294920 | tf_op jit(solution)/shard_map/ppermute | solution.py:156
  70.6 8.4 %collective-permute-start.20 = (f32[2,96,128]{2,1,0:T(8,128)S(1)}, f32[2,96,128]{2,1,0:T(8,128)S(1)}, u32[]{:S(2)}, u32[]{:S(2)}) collective-permute-start(f32[2,96,128]{2,1,0:T(8,128)S(1)} %bitcast.40), channel_id=1, source_target_pairs={{0,2},{1,15},{2,4},{3,1},{4,6},{5,3},{6,8},{7,5},{8,10},{9,7},{10,... | collective-permute-start | bytes 294920 | tf_op jit(solution)/shard_map/ppermute | solution.py:156
  71.5 8.7 %collective-permute-start.19 = (f32[96,128]{1,0:T(8,128)S(1)}, f32[96,128]{1,0:T(8,128)S(1)}, u32[]{:S(2)}, u32[]{:S(2)}) collective-permute-start(f32[96,128]{1,0:T(8,128)S(1)} %slice.96), channel_id=1, source_target_pairs={{0,8},{1,9},{2,10},{3,11},{4,12},{5,13},{6,14},{7,15},{8,0},{9,1},... | collective-permute-start | bytes 147464 | tf_op jit(solution)/shard_map/ppermute | solution.py:157
  79.1 2.0 %collective-permute-start.23 = (f32[96,128]{1,0:T(8,128)S(1)}, f32[96,128]{1,0:T(8,128)S(1)}, u32[]{:S(2)}, u32[]{:S(2)}) collective-permute-start(f32[96,128]{1,0:T(8,128)S(1)} %fusion.6), channel_id=1, source_target_pairs={{0,1},{1,0},{2,3},{3,2},{4,5},{5,4},{6,7},{7,6},{8,9},{9,8},{10,11... | collective-permute-start | bytes 147464 | tf_op jit(solution)/shard_map/ppermute | solution.py:162

commit v3 on v2

--- a/solution.py
+++ b/solution.py
@@ -20,19 +20,16 @@
     owners = matrix_ref.shape[1] // piece
     width = ROUND * piece
     rounds = [(i, j) for i in range(count // ROUND) for j in range(owners // ROUND)]
-    arriving = {}
+    arriving = []
+    for n in range(count):
+        there = pl.ds(pl.multiple_of(source_ref[first + n] * piece, piece), piece)
+        copy = pltpu.make_async_copy(matrix_hbm.at[there, :], matrix_ref.at[pl.ds(n * piece, piece), :], sems.at[n])
+        copy.start()
+        arriving.append(copy)
     for i, j in rounds:
-        across = pl.ds(j * width, width)
-        for n in range(i * ROUND, (i + 1) * ROUND):
-            there = pl.ds(pl.multiple_of(source_ref[first + n] * piece, piece), piece)
-            copy = pltpu.make_async_copy(
-                matrix_hbm.at[there, across], matrix_ref.at[pl.ds(n * piece, piece), across], sems.at[n, j]
-            )
-            copy.start()
-            arriving[n, j] = copy
-    for i, j in rounds:
-        for n in range(i * ROUND, (i + 1) * ROUND):
-            arriving[n, j].wait()
+        if j == 0:
+            for copy in arriving[i * ROUND : (i + 1) * ROUND]:
+                copy.wait()
         cols = slice(i * width, (i + 1) * width)
         turned = matrix_ref[cols, j * width : (j + 1) * width].T
         for k in range(ROUND):
@@ -54,10 +51,31 @@
         in_specs=[scalars, scalars, pl.BlockSpec(memory_space=pltpu.HBM)],
         out_specs=[on_chip, on_chip],
         out_shape=[out, out],
-        scratch_shapes=[pltpu.VMEM((depth, rows), jnp.float32), pltpu.SemaphoreType.DMA((count, rows // (ROUND * piece)))],
+        scratch_shapes=[pltpu.VMEM((depth, rows), jnp.float32), pltpu.SemaphoreType.DMA((count,))],
         compiler_params=pltpu.CompilerParams(vmem_limit_bytes=VMEM_LIMIT),
         name="split_matrix",
     )(slots, sources, pltpu.with_memory_space_constraint(columns, pltpu.HBM))
+
+
+def hold_kernel(part_ref, held_ref):
+    held_ref[...] = part_ref[...]
+
+
+def bundle_kernel(*refs):
+    rows = refs[0].shape[0]
+    for n, ref in enumerate(refs[:-1]):
+        refs[-1][n * rows : (n + 1) * rows, :] = ref[...]
+
+
+def on_chip_call(kernel, out, name, *operands):
+    on_chip = pl.BlockSpec(memory_space=pltpu.VMEM)
+    return pl.pallas_call(kernel, in_specs=[on_chip] * len(operands), out_specs=on_chip, out_shape=out, name=name, compiler_params=pltpu.CompilerParams(vmem_limit_bytes=2**20))(*operands)
+
+
+def bundle(part, others):
+    rows, width = others[0].shape
+    out = jax.ShapeDtypeStruct((rows * (1 + len(others)), width), others[0].dtype)
+    return on_chip_call(bundle_kernel, out, "bundle", part, *others)
 
 
 def product_kernel(*refs, half, parts):
@@ -171,11 +189,12 @@
     slots, order, core_row = lax.optimization_barrier((slots_here(), sources_here(), core_row))
     part = sources.reshape(piece, width)
     others = first_round(part)
+    part = on_chip_call(hold_kernel, pltpu.VMEM(part.shape, part.dtype), "hold", part)
     count = columns.shape[0] // piece // PARTS
     matrix = []
     results = []
     for step in range(2):
-        gathered = second_round(jnp.concatenate([part] + list(others), axis=0))
+        gathered = second_round(bundle(part, others))
         for n in range(len(matrix) // 2, PARTS):
             matrix = matrix + list(split_matrix(slots, order, columns, piece, n * count, count))
         theirs = product(matrix, gathered, 1)

time: 81.9 us -> 79.5 us (0.971)
  waiting for transfers between devices: 23.2 us -> 21.9 us
  Pallas kernels: 11.8 us -> 10.8 us
  local copies, waits for them, and re-layouts: 0.06 us -> 0.89 us
  other arithmetic: 1.65 us -> 0.83 us
    ppermute x6, waiting for transfers between devices: 7.82 us -> 6.61 us  [first_round(): lax.ppermute(part, ('row', 'depth'), gather_pairs(True, shift))]
    pallas_call x1, Pallas kernels: 6.31 us -> 5.21 us  [split_matrix(): pl.pallas_call(functools.partial(split_kernel, piece=piece, first=first),...]
    unnamed x2 -> x4, local copies, waits for them, and re-layouts: 0.01 us -> 0.84 us
    concatenate x2 -> x0, other arithmetic: 0.83 us -> none  [body(): gathered = second_round(jnp.concatenate([part] + list(others), axis=0))]
  transfers between devices with their start and end apart: 24 -> 24, of which waited for: 14 -> 12; matrix products, arithmetic and copies ran while one was open for 0% -> 0% of each run, Pallas kernels for 11% -> 10%
where the time goes in v3:
time: 79.5 us; the launch traced here: 79.4 us
  starting transfers between devices  44.2 us (56%)
  waiting for transfers between devices  21.9 us (28%)
  Pallas kernels  10.8 us (14%)
  local copies, waits for them, and re-layouts  0.89 us (1%)
  other arithmetic  0.83 us (1%)
  between operations  0.81 us (1%)
    ppermute x6, starting transfers between devices, to_owners(): lax.ppermute(summed[2 * (hops - 1):2 * hops], axes, pairs(hops))  11.3 us
    ppermute x2, starting transfers between devices, to_owners(): opposite = lax.ppermute(summed[ring - 2], axes, pairs(half))  8.4 us
    ppermute x6, starting transfers between devices, first_round(): lax.ppermute(part, ('row', 'depth'), gather_pairs(True, shift))  7.92 us
    ppermute x2, starting transfers between devices, to_owners(): received = lax.ppermute(theirs, 'depth', SWAP)  7.51 us
    ppermute x6, waiting for transfers between devices, to_owners(): lax.ppermute(summed[2 * (hops - 1):2 * hops], axes, pairs(hops))  6.91 us
    ppermute x6, waiting for transfers between devices, second_round(): lax.ppermute(line, ('row', 'depth'), gather_pairs(False, shift))  6.65 us
    ppermute x6, waiting for transfers between devices, first_round(): lax.ppermute(part, ('row', 'depth'), gather_pairs(True, shift))  6.61 us
    ppermute x6, starting transfers between devices, second_round(): lax.ppermute(line, ('row', 'depth'), gather_pairs(False, shift))  6.16 us
  transfers between devices with their start and end apart: 24, of which 12 were waited for; matrix products, arithmetic and copies ran while one was open for 0% of the time, Pallas kernels for 10%

profile of v3, /device:TPU:1, one launch (start us, length us, event | category | flops | bytes accessed | tf_op | source)
XLA Modules:
  0.0 79.4 jit_solution(16474153202569639367)
XLA Ops:
  0.6 3.8 %collective-permute-start.2 = (f32[96,128]{1,0:T(8,128)}, f32[96,128]{1,0:T(8,128)S(1)}, u32[]{:S(2)}, u32[]{:S(2)}) collective-permute-start(f32[96,128]{1,0:T(8,128)} %bitcast.38), channel_id=1, source_target_pairs={{0,32},{1,129},{16,48},{17,145},{32,0},{33,161},{48,16},{49,177},{... | collective-permute-start | bytes 147464 | tf_op jit(solution)/shard_map/ppermute | solution.py:124
  4.5 0.8 collective-permute-start.1
  5.2 0.7 collective-permute-start
  5.9 0.0 copy-start.1
  5.9 0.8 %copy-done.1 = f32[1,1,96,128]{3,2,1,0:T(8,128)S(1)} copy-done((f32[1,1,96,128]{3,2,1,0:T(8,128)S(1)}, f32[1,1,96,128]{3,2,1,0:T(8,128)}, u32[]{:S(2)}) %copy-start.1) | copy-done | bytes 49176
  6.8 0.0 collective-permute-done.2.refs_3_
  6.8 0.8 %collective-permute-done.1.refs_2_ = f32[96,128]{1,0:T(8,128)S(1)} collective-permute-done((f32[96,128]{1,0:T(8,128)}, f32[96,128]{1,0:T(8,128)S(1)}, u32[]{:S(2)}, u32[]{:S(2)}) %collective-permute-start.1) | collective-permute-done | bytes 49184 | tf_op jit(solution)/shard_map/ppermute | solution.py:124
  7.6 2.0 %collective-permute-done.refs_1_ = f32[96,128]{1,0:T(8,128)S(1)} collective-permute-done((f32[96,128]{1,0:T(8,128)}, f32[96,128]{1,0:T(8,128)S(1)}, u32[]{:S(2)}, u32[]{:S(2)}) %collective-permute-start) | collective-permute-done | bytes 49184 | tf_op jit(solution)/shard_map/ppermute | solution.py:124
  9.6 2.8 %collective-permute-start.5 = (f32[384,128]{1,0:T(8,128)S(1)}, f32[384,128]{1,0:T(8,128)S(1)}, u32[]{:S(2)}, u32[]{:S(2)}) collective-permute-start(f32[384,128]{1,0:T(8,128)S(1)} %bundle.2.refs_2_), channel_id=1, source_target_pairs={{0,128},{1,33},{16,144},{17,49},{32,160},{33,1},{48,176},{49,17},{... | collective-permute-start | bytes 589832 | tf_op jit(solution)/shard_map/ppermute | solution.py:128
  12.4 0.9 %collective-permute-start.4 = (f32[384,128]{1,0:T(8,128)S(1)}, f32[384,128]{1,0:T(8,128)S(1)}, u32[]{:S(2)}, u32[]{:S(2)}) collective-permute-start(f32[384,128]{1,0:T(8,128)S(1)} %bundle.2.refs_2_), channel_id=1, source_target_pairs={{0,192},{1,49},{16,208},{17,1},{32,224},{33,17},{48,240},{49,33},{... | collective-permute-start | bytes 589832 | tf_op jit(solution)/shard_map/ppermute | solution.py:128
  13.3 0.6 collective-permute-start.3
  13.9 5.2 %split_matrix.1 = (bf16[1536,1536]{1,0:T(8,128)(2,1)S(1)}, bf16[1536,1536]{1,0:T(8,128)(2,1)S(1)}) custom-call(s32[16]{0:T(128)S(1)} %get-tuple-element.7.slot_ref, s32[16]{0:T(128)S(1)} %get-tuple-element.8.source_ref, f32[1536,1536]{1,0:T(8,128)} %bitcast.42), custom_call_target="tpu_custom_call" | custom-call | tf_op jit(solution)/shard_map/split_matrix/pallas_call | solution.py:49
  19.2 0.0 collective-permute-done.5.refs_5_
  19.2 0.0 collective-permute-done.4.refs_4_
  19.2 0.0 collective-permute-done.3.refs_3_
  19.2 1.4 %product.5 = f32[768,128]{1,0:T(8,128)S(1)} custom-call(bf16[1536,1536]{1,0:T(8,128)(2,1)S(1)} %get-tuple-element.9.refs_0_, bf16[1536,1536]{1,0:T(8,128)(2,1)S(1)} %get-tuple-element.10.refs_1_, f32[384,128]{1,0:T(8,128)S(1)} %bundle.2.refs_2_, f32[384,128]{1,0:T(8,128)S(1)} %collective-permute-done.3.refs_3_, ...), custom_call_target="tpu_custom_call" | custom-call | tf_op jit(solution)/shard_map/product/pallas_call | solution.py:102
  20.6 4.0 %collective-permute-start.6 = (f32[768,128]{1,0:T(8,128)S(1)}, f32[768,128]{1,0:T(8,128)S(1)}, u32[]{:S(2)}, u32[]{:S(2)}) collective-permute-start(f32[768,128]{1,0:T(8,128)S(1)} %product.5), channel_id=1, source_target_pairs={{0,1},{1,0},{2,3},{3,2},{4,5},{5,4},{6,7},{7,6},{8,9},{9,8},{10,11... | collective-permute-start | bytes 1179656 | tf_op jit(solution)/shard_map/ppermute | solution.py:164
  24.6 1.4 %product.4 = f32[768,128]{1,0:T(8,128)S(1)} custom-call(bf16[1536,1536]{1,0:T(8,128)(2,1)S(1)} %get-tuple-element.9.refs_0_, bf16[1536,1536]{1,0:T(8,128)(2,1)S(1)} %get-tuple-element.10.refs_1_, f32[384,128]{1,0:T(8,128)S(1)} %bundle.2.refs_2_, f32[384,128]{1,0:T(8,128)S(1)} %collective-permute-done.3.refs_3_, ...), custom_call_target="tpu_custom_call" | custom-call | tf_op jit(solution)/shard_map/product/pallas_call | solution.py:102
  26.0 0.0 collective-permute-done.6
  26.0 0.1 add.74
  26.1 6.5 %collective-permute-start.10 = (f32[2,96,128]{2,1,0:T(8,128)S(1)}, f32[2,96,128]{2,1,0:T(8,128)S(1)}, u32[]{:S(2)}, u32[]{:S(2)}) collective-permute-start(f32[2,96,128]{2,1,0:T(8,128)S(1)} %bitcast.47), channel_id=1, source_target_pairs={{0,6},{1,11},{2,8},{3,13},{4,10},{5,15},{6,12},{7,1},{8,14},{9,3},... | collective-permute-start | bytes 294920 | tf_op jit(solution)/shard_map/ppermute | solution.py:174
  32.6 0.3 collective-permute-start.9
  32.9 0.5 collective-permute-start.8
  33.4 4.7 %collective-permute-start.7 = (f32[96,128]{1,0:T(8,128)S(1)}, f32[96,128]{1,0:T(8,128)S(1)}, u32[]{:S(2)}, u32[]{:S(2)}) collective-permute-start(f32[96,128]{1,0:T(8,128)S(1)} %slice.89), channel_id=1, source_target_pairs={{0,8},{1,9},{2,10},{3,11},{4,12},{5,13},{6,14},{7,15},{8,0},{9,1},... | collective-permute-start | bytes 147464 | tf_op jit(solution)/shard_map/ppermute | solution.py:175
  38.1 0.0 collective-permute-done.10
  38.1 0.7 collective-permute-done.9
  38.9 2.2 %collective-permute-done.8 = f32[2,96,128]{2,1,0:T(8,128)S(1)} collective-permute-done((f32[2,96,128]{2,1,0:T(8,128)S(1)}, f32[2,96,128]{2,1,0:T(8,128)S(1)}, u32[]{:S(2)}, u32[]{:S(2)}) %collective-permute-start.8) | collective-permute-done | bytes 98336 | tf_op jit(solution)/shard_map/ppermute | solution.py:174
  41.1 2.2 %collective-permute-start.11 = (f32[96,128]{1,0:T(8,128)S(1)}, f32[96,128]{1,0:T(8,128)S(1)}, u32[]{:S(2)}, u32[]{:S(2)}) collective-permute-start(f32[96,128]{1,0:T(8,128)S(1)} %fusion.5), channel_id=1, source_target_pairs={{0,1},{1,0},{2,3},{3,2},{4,5},{5,4},{6,7},{7,6},{8,9},{9,8},{10,11... | collective-permute-start | bytes 147464 | tf_op jit(solution)/shard_map/ppermute | solution.py:180
  43.3 0.0 collective-permute-done.7
  43.3 0.9 %collective-permute-done.11 = f32[96,128]{1,0:T(8,128)S(1)} collective-permute-done((f32[96,128]{1,0:T(8,128)S(1)}, f32[96,128]{1,0:T(8,128)S(1)}, u32[]{:S(2)}, u32[]{:S(2)}) %collective-permute-start.11) | collective-permute-done | bytes 49184 | tf_op jit(solution)/shard_map/ppermute | solution.py:180
  44.2 0.0 copy-start
  44.2 1.2 %collective-permute-start.14 = (f32[96,128]{1,0:T(8,128)S(1)}, f32[96,128]{1,0:T(8,128)S(1)}, u32[]{:S(2)}, u32[]{:S(2)}) collective-permute-start(f32[96,128]{1,0:T(8,128)S(1)} %fusion.4.refs_0_), channel_id=1, source_target_pairs={{0,32},{1,129},{16,48},{17,145},{32,0},{33,161},{48,16},{49,177},{... | collective-permute-start | bytes 147464 | tf_op jit(solution)/shard_map/ppermute | solution.py:124
  45.4 1.1 %collective-permute-start.13 = (f32[96,128]{1,0:T(8,128)S(1)}, f32[96,128]{1,0:T(8,128)S(1)}, u32[]{:S(2)}, u32[]{:S(2)}) collective-permute-start(f32[96,128]{1,0:T(8,128)S(1)} %fusion.4.refs_0_), channel_id=1, source_target_pairs={{0,48},{1,193},{16,0},{17,209},{32,16},{33,225},{48,32},{49,241},{... | collective-permute-start | bytes 147464 | tf_op jit(solution)/shard_map/ppermute | solution.py:124
  46.5 0.4 collective-permute-start.12
  46.9 1.9 %collective-permute-done.14.refs_3_ = f32[96,128]{1,0:T(8,128)S(1)} collective-permute-done((f32[96,128]{1,0:T(8,128)S(1)}, f32[96,128]{1,0:T(8,128)S(1)}, u32[]{:S(2)}, u32[]{:S(2)}) %collective-permute-start.14) | collective-permute-done | bytes 49184 | tf_op jit(solution)/shard_map/ppermute | solution.py:124
  48.8 0.0 collective-permute-done.13.refs_2_
  48.8 1.9 %collective-permute-done.12.refs_1_ = f32[96,128]{1,0:T(8,128)S(1)} collective-permute-done((f32[96,128]{1,0:T(8,128)S(1)}, f32[96,128]{1,0:T(8,128)S(1)}, u32[]{:S(2)}, u32[]{:S(2)}) %collective-permute-start.12) | collective-permute-done | bytes 49184 | tf_op jit(solution)/shard_map/ppermute | solution.py:124
  50.7 0.1 collective-permute-start.17
  50.8 1.8 %collective-permute-start.16 = (f32[384,128]{1,0:T(8,128)S(1)}, f32[384,128]{1,0:T(8,128)S(1)}, u32[]{:S(2)}, u32[]{:S(2)}) collective-permute-start(f32[384,128]{1,0:T(8,128)S(1)} %bundle.3.refs_2_), channel_id=1, source_target_pairs={{0,192},{1,49},{16,208},{17,1},{32,224},{33,17},{48,240},{49,33},{... | collective-permute-start | bytes 589832 | tf_op jit(solution)/shard_map/ppermute | solution.py:128
  52.5 0.0 collective-permute-start.15
  52.5 4.3 %collective-permute-done.17.refs_5_ = f32[384,128]{1,0:T(8,128)S(1)} collective-permute-done((f32[384,128]{1,0:T(8,128)S(1)}, f32[384,128]{1,0:T(8,128)S(1)}, u32[]{:S(2)}, u32[]{:S(2)}) %collective-permute-start.17) | collective-permute-done | bytes 196640 | tf_op jit(solution)/shard_map/ppermute | solution.py:128
  56.8 0.0 collective-permute-done.16.refs_4_
  56.8 2.3 %collective-permute-done.15.refs_3_ = f32[384,128]{1,0:T(8,128)S(1)} collective-permute-done((f32[384,128]{1,0:T(8,128)S(1)}, f32[384,128]{1,0:T(8,128)S(1)}, u32[]{:S(2)}, u32[]{:S(2)}) %collective-permute-start.15) | collective-permute-done | bytes 196640 | tf_op jit(solution)/shard_map/ppermute | solution.py:128
  59.2 1.4 %product.7 = f32[768,128]{1,0:T(8,128)S(1)} custom-call(bf16[1536,1536]{1,0:T(8,128)(2,1)S(1)} %get-tuple-element.9.refs_0_, bf16[1536,1536]{1,0:T(8,128)(2,1)S(1)} %get-tuple-element.10.refs_1_, f32[384,128]{1,0:T(8,128)S(1)} %bundle.3.refs_2_, f32[384,128]{1,0:T(8,128)S(1)} %collective-permute-done.15.refs_3_, ...), custom_call_target="tpu_custom_call" | custom-call | tf_op jit(solution)/shard_map/product/pallas_call | solution.py:102
  60.6 0.0 copy-done
  60.6 3.5 %collective-permute-start.18 = (f32[768,128]{1,0:T(8,128)S(1)}, f32[768,128]{1,0:T(8,128)S(1)}, u32[]{:S(2)}, u32[]{:S(2)}) collective-permute-start(f32[768,128]{1,0:T(8,128)S(1)} %product.7), channel_id=1, source_target_pairs={{0,1},{1,0},{2,3},{3,2},{4,5},{5,4},{6,7},{7,6},{8,9},{9,8},{10,11... | collective-permute-start | bytes 1179656 | tf_op jit(solution)/shard_map/ppermute | solution.py:164
  64.1 1.4 %product.6 = f32[768,128]{1,0:T(8,128)S(1)} custom-call(bf16[1536,1536]{1,0:T(8,128)(2,1)S(1)} %get-tuple-element.9.refs_0_, bf16[1536,1536]{1,0:T(8,128)(2,1)S(1)} %get-tuple-element.10.refs_1_, f32[384,128]{1,0:T(8,128)S(1)} %bundle.3.refs_2_, f32[384,128]{1,0:T(8,128)S(1)} %collective-permute-done.15.refs_3_, ...), custom_call_target="tpu_custom_call" | custom-call | tf_op jit(solution)/shard_map/product/pallas_call | solution.py:102
  65.4 0.0 collective-permute-done.18
  65.5 1.4 %collective-permute-start.22 = (f32[2,96,128]{2,1,0:T(8,128)S(1)}, f32[2,96,128]{2,1,0:T(8,128)S(1)}, u32[]{:S(2)}, u32[]{:S(2)}) collective-permute-start(f32[2,96,128]{2,1,0:T(8,128)S(1)} %bitcast.48), channel_id=1, source_target_pairs={{0,6},{1,11},{2,8},{3,13},{4,10},{5,15},{6,12},{7,1},{8,14},{9,3},... | collective-permute-start | bytes 294920 | tf_op jit(solution)/shard_map/ppermute | solution.py:174
  67.0 2.1 %collective-permute-start.21 = (f32[2,96,128]{2,1,0:T(8,128)S(1)}, f32[2,96,128]{2,1,0:T(8,128)S(1)}, u32[]{:S(2)}, u32[]{:S(2)}) collective-permute-start(f32[2,96,128]{2,1,0:T(8,128)S(1)} %bitcast.46), channel_id=1, source_target_pairs={{0,4},{1,13},{2,6},{3,15},{4,8},{5,1},{6,10},{7,3},{8,12},{9,5},{1... | collective-permute-start | bytes 294920 | tf_op jit(solution)/shard_map/ppermute | solution.py:174
  69.1 0.5 collective-permute-start.20
  69.5 3.7 %collective-permute-start.19 = (f32[96,128]{1,0:T(8,128)S(1)}, f32[96,128]{1,0:T(8,128)S(1)}, u32[]{:S(2)}, u32[]{:S(2)}) collective-permute-start(f32[96,128]{1,0:T(8,128)S(1)} %slice.96), channel_id=1, source_target_pairs={{0,8},{1,9},{2,10},{3,11},{4,12},{5,13},{6,14},{7,15},{8,0},{9,1},... | collective-permute-start | bytes 147464 | tf_op jit(solution)/shard_map/ppermute | solution.py:175
  73.2 0.0 collective-permute-done.22
  73.2 1.9 %collective-permute-done.21 = f32[2,96,128]{2,1,0:T(8,128)S(1)} collective-permute-done((f32[2,96,128]{2,1,0:T(8,128)S(1)}, f32[2,96,128]{2,1,0:T(8,128)S(1)}, u32[]{:S(2)}, u32[]{:S(2)}) %collective-permute-start.21) | collective-permute-done | bytes 98336 | tf_op jit(solution)/shard_map/ppermute | solution.py:174
  75.1 2.1 %collective-permute-done.20 = f32[2,96,128]{2,1,0:T(8,128)S(1)} collective-permute-done((f32[2,96,128]{2,1,0:T(8,128)S(1)}, f32[2,96,128]{2,1,0:T(8,128)S(1)}, u32[]{:S(2)}, u32[]{:S(2)}) %collective-permute-start.20) | collective-permute-done | bytes 98336 | tf_op jit(solution)/shard_map/ppermute | solution.py:174
  77.2 0.7 collective-permute-start.23
  77.9 0.0 collective-permute-done.19
  77.9 0.9 %collective-permute-done.23 = f32[96,128]{1,0:T(8,128)S(1)} collective-permute-done((f32[96,128]{1,0:T(8,128)S(1)}, f32[96,128]{1,0:T(8,128)S(1)}, u32[]{:S(2)}, u32[]{:S(2)}) %collective-permute-start.23) | collective-permute-done | bytes 49184 | tf_op jit(solution)/shard_map/ppermute | solution.py:180
  78.8 0.6 fusion.2
  (16 shorter events, 0.2 us)
Async XLA Ops:
  0.6 6.1 %collective-permute-start.2 = (f32[96,128]{1,0:T(8,128)}, f32[96,128]{1,0:T(8,128)S(1)}, u32[]{:S(2)}, u32[]{:S(2)}) collective-permute-start(f32[96,128]{1,0:T(8,128)} %bitcast.38), channel_id=1, source_target_pairs={{0,32},{1,129},{16,48},{17,145},{32,0},{33,161},{48,16},{49,177},{... | collective-permute-start | bytes 147464 | tf_op jit(solution)/shard_map/ppermute | solution.py:124
  4.5 3.2 %collective-permute-start.1 = (f32[96,128]{1,0:T(8,128)}, f32[96,128]{1,0:T(8,128)S(1)}, u32[]{:S(2)}, u32[]{:S(2)}) collective-permute-start(f32[96,128]{1,0:T(8,128)} %bitcast.39), channel_id=1, source_target_pairs={{0,48},{1,193},{16,0},{17,209},{32,16},{33,225},{48,32},{49,241},{... | collective-permute-start | bytes 147464 | tf_op jit(solution)/shard_map/ppermute | solution.py:124
  5.2 4.4 %collective-permute-start = (f32[96,128]{1,0:T(8,128)}, f32[96,128]{1,0:T(8,128)S(1)}, u32[]{:S(2)}, u32[]{:S(2)}) collective-permute-start(f32[96,128]{1,0:T(8,128)} %bitcast.40), channel_id=1, source_target_pairs={{0,16},{1,65},{16,32},{17,81},{32,48},{33,97},{48,0},{49,113},{64,... | collective-permute-start | bytes 147464 | tf_op jit(solution)/shard_map/ppermute | solution.py:124
  5.9 0.8 %copy-start.1 = (f32[1,1,96,128]{3,2,1,0:T(8,128)S(1)}, f32[1,1,96,128]{3,2,1,0:T(8,128)}, u32[]{:S(2)}) copy-start(f32[1,1,96,128]{3,2,1,0:T(8,128)} %param.3) | copy-start | bytes 147460
  9.6 9.5 %collective-permute-start.5 = (f32[384,128]{1,0:T(8,128)S(1)}, f32[384,128]{1,0:T(8,128)S(1)}, u32[]{:S(2)}, u32[]{:S(2)}) collective-permute-start(f32[384,128]{1,0:T(8,128)S(1)} %bundle.2.refs_2_), channel_id=1, source_target_pairs={{0,128},{1,33},{16,144},{17,49},{32,160},{33,1},{48,176},{49,17},{... | collective-permute-start | bytes 589832 | tf_op jit(solution)/shard_map/ppermute | solution.py:128
  12.4 6.7 %collective-permute-start.4 = (f32[384,128]{1,0:T(8,128)S(1)}, f32[384,128]{1,0:T(8,128)S(1)}, u32[]{:S(2)}, u32[]{:S(2)}) collective-permute-start(f32[384,128]{1,0:T(8,128)S(1)} %bundle.2.refs_2_), channel_id=1, source_target_pairs={{0,192},{1,49},{16,208},{17,1},{32,224},{33,17},{48,240},{49,33},{... | collective-permute-start | bytes 589832 | tf_op jit(solution)/shard_map/ppermute | solution.py:128
  13.3 5.9 %collective-permute-start.3 = (f32[384,128]{1,0:T(8,128)S(1)}, f32[384,128]{1,0:T(8,128)S(1)}, u32[]{:S(2)}, u32[]{:S(2)}) collective-permute-start(f32[384,128]{1,0:T(8,128)S(1)} %bundle.2.refs_2_), channel_id=1, source_target_pairs={{0,64},{1,17},{16,80},{17,33},{32,96},{33,49},{48,112},{49,1},{64,... | collective-permute-start | bytes 589832 | tf_op jit(solution)/shard_map/ppermute | solution.py:128
  20.6 5.4 %collective-permute-start.6 = (f32[768,128]{1,0:T(8,128)S(1)}, f32[768,128]{1,0:T(8,128)S(1)}, u32[]{:S(2)}, u32[]{:S(2)}) collective-permute-start(f32[768,128]{1,0:T(8,128)S(1)} %product.5), channel_id=1, source_target_pairs={{0,1},{1,0},{2,3},{3,2},{4,5},{5,4},{6,7},{7,6},{8,9},{9,8},{10,11... | collective-permute-start | bytes 1179656 | tf_op jit(solution)/shard_map/ppermute | solution.py:164
  26.1 12.0 %collective-permute-start.10 = (f32[2,96,128]{2,1,0:T(8,128)S(1)}, f32[2,96,128]{2,1,0:T(8,128)S(1)}, u32[]{:S(2)}, u32[]{:S(2)}) collective-permute-start(f32[2,96,128]{2,1,0:T(8,128)S(1)} %bitcast.47), channel_id=1, source_target_pairs={{0,6},{1,11},{2,8},{3,13},{4,10},{5,15},{6,12},{7,1},{8,14},{9,3},... | collective-permute-start | bytes 294920 | tf_op jit(solution)/shard_map/ppermute | solution.py:174
  32.6 6.2 %collective-permute-start.9 = (f32[2,96,128]{2,1,0:T(8,128)S(1)}, f32[2,96,128]{2,1,0:T(8,128)S(1)}, u32[]{:S(2)}, u32[]{:S(2)}) collective-permute-start(f32[2,96,128]{2,1,0:T(8,128)S(1)} %bitcast.45), channel_id=1, source_target_pairs={{0,4},{1,13},{2,6},{3,15},{4,8},{5,1},{6,10},{7,3},{8,12},{9,5},{1... | collective-permute-start | bytes 294920 | tf_op jit(solution)/shard_map/ppermute | solution.py:174
  32.9 8.1 %collective-permute-start.8 = (f32[2,96,128]{2,1,0:T(8,128)S(1)}, f32[2,96,128]{2,1,0:T(8,128)S(1)}, u32[]{:S(2)}, u32[]{:S(2)}) collective-permute-start(f32[2,96,128]{2,1,0:T(8,128)S(1)} %bitcast.43), channel_id=1, source_target_pairs={{0,2},{1,15},{2,4},{3,1},{4,6},{5,3},{6,8},{7,5},{8,10},{9,7},{10,... | collective-permute-start | bytes 294920 | tf_op jit(solution)/shard_map/ppermute | solution.py:174
  33.4 9.9 %collective-permute-start.7 = (f32[96,128]{1,0:T(8,128)S(1)}, f32[96,128]{1,0:T(8,128)S(1)}, u32[]{:S(2)}, u32[]{:S(2)}) collective-permute-start(f32[96,128]{1,0:T(8,128)S(1)} %slice.89), channel_id=1, source_target_pairs={{0,8},{1,9},{2,10},{3,11},{4,12},{5,13},{6,14},{7,15},{8,0},{9,1},... | collective-permute-start | bytes 147464 | tf_op jit(solution)/shard_map/ppermute | solution.py:175
  41.1 3.1 %collective-permute-start.11 = (f32[96,128]{1,0:T(8,128)S(1)}, f32[96,128]{1,0:T(8,128)S(1)}, u32[]{:S(2)}, u32[]{:S(2)}) collective-permute-start(f32[96,128]{1,0:T(8,128)S(1)} %fusion.5), channel_id=1, source_target_pairs={{0,1},{1,0},{2,3},{3,2},{4,5},{5,4},{6,7},{7,6},{8,9},{9,8},{10,11... | collective-permute-start | bytes 147464 | tf_op jit(solution)/shard_map/ppermute | solution.py:180
  44.2 16.3 %copy-start = (f32[96,128]{1,0:T(8,128)}, f32[96,128]{1,0:T(8,128)S(1)}, u32[]{:S(2)}) copy-start(f32[96,128]{1,0:T(8,128)S(1)} %fusion.4.refs_0_) | copy-start | bytes 147460
  44.2 4.5 %collective-permute-start.14 = (f32[96,128]{1,0:T(8,128)S(1)}, f32[96,128]{1,0:T(8,128)S(1)}, u32[]{:S(2)}, u32[]{:S(2)}) collective-permute-start(f32[96,128]{1,0:T(8,128)S(1)} %fusion.4.refs_0_), channel_id=1, source_target_pairs={{0,32},{1,129},{16,48},{17,145},{32,0},{33,161},{48,16},{49,177},{... | collective-permute-start | bytes 147464 | tf_op jit(solution)/shard_map/ppermute | solution.py:124
  45.4 3.4 %collective-permute-start.13 = (f32[96,128]{1,0:T(8,128)S(1)}, f32[96,128]{1,0:T(8,128)S(1)}, u32[]{:S(2)}, u32[]{:S(2)}) collective-permute-start(f32[96,128]{1,0:T(8,128)S(1)} %fusion.4.refs_0_), channel_id=1, source_target_pairs={{0,48},{1,193},{16,0},{17,209},{32,16},{33,225},{48,32},{49,241},{... | collective-permute-start | bytes 147464 | tf_op jit(solution)/shard_map/ppermute | solution.py:124
  46.5 4.2 %collective-permute-start.12 = (f32[96,128]{1,0:T(8,128)S(1)}, f32[96,128]{1,0:T(8,128)S(1)}, u32[]{:S(2)}, u32[]{:S(2)}) collective-permute-start(f32[96,128]{1,0:T(8,128)S(1)} %fusion.4.refs_0_), channel_id=1, source_target_pairs={{0,16},{1,65},{16,32},{17,81},{32,48},{33,97},{48,0},{49,113},{64,... | collective-permute-start | bytes 147464 | tf_op jit(solution)/shard_map/ppermute | solution.py:124
  50.7 6.2 %collective-permute-start.17 = (f32[384,128]{1,0:T(8,128)S(1)}, f32[384,128]{1,0:T(8,128)S(1)}, u32[]{:S(2)}, u32[]{:S(2)}) collective-permute-start(f32[384,128]{1,0:T(8,128)S(1)} %bundle.3.refs_2_), channel_id=1, source_target_pairs={{0,128},{1,33},{16,144},{17,49},{32,160},{33,1},{48,176},{49,17},{... | collective-permute-start | bytes 589832 | tf_op jit(solution)/shard_map/ppermute | solution.py:128
  50.8 6.1 %collective-permute-start.16 = (f32[384,128]{1,0:T(8,128)S(1)}, f32[384,128]{1,0:T(8,128)S(1)}, u32[]{:S(2)}, u32[]{:S(2)}) collective-permute-start(f32[384,128]{1,0:T(8,128)S(1)} %bundle.3.refs_2_), channel_id=1, source_target_pairs={{0,192},{1,49},{16,208},{17,1},{32,224},{33,17},{48,240},{49,33},{... | collective-permute-start | bytes 589832 | tf_op jit(solution)/shard_map/ppermute | solution.py:128
  52.5 6.6 %collective-permute-start.15 = (f32[384,128]{1,0:T(8,128)S(1)}, f32[384,128]{1,0:T(8,128)S(1)}, u32[]{:S(2)}, u32[]{:S(2)}) collective-permute-start(f32[384,128]{1,0:T(8,128)S(1)} %bundle.3.refs_2_), channel_id=1, source_target_pairs={{0,64},{1,17},{16,80},{17,33},{32,96},{33,49},{48,112},{49,1},{64,... | collective-permute-start | bytes 589832 | tf_op jit(solution)/shard_map/ppermute | solution.py:128
  60.6 4.9 %collective-permute-start.18 = (f32[768,128]{1,0:T(8,128)S(1)}, f32[768,128]{1,0:T(8,128)S(1)}, u32[]{:S(2)}, u32[]{:S(2)}) collective-permute-start(f32[768,128]{1,0:T(8,128)S(1)} %product.7), channel_id=1, source_target_pairs={{0,1},{1,0},{2,3},{3,2},{4,5},{5,4},{6,7},{7,6},{8,9},{9,8},{10,11... | collective-permute-start | bytes 1179656 | tf_op jit(solution)/shard_map/ppermute | solution.py:164
  65.5 7.6 %collective-permute-start.22 = (f32[2,96,128]{2,1,0:T(8,128)S(1)}, f32[2,96,128]{2,1,0:T(8,128)S(1)}, u32[]{:S(2)}, u32[]{:S(2)}) collective-permute-start(f32[2,96,128]{2,1,0:T(8,128)S(1)} %bitcast.48), channel_id=1, source_target_pairs={{0,6},{1,11},{2,8},{3,13},{4,10},{5,15},{6,12},{7,1},{8,14},{9,3},... | collective-permute-start | bytes 294920 | tf_op jit(solution)/shard_map/ppermute | solution.py:174
  67.0 8.1 %collective-permute-start.21 = (f32[2,96,128]{2,1,0:T(8,128)S(1)}, f32[2,96,128]{2,1,0:T(8,128)S(1)}, u32[]{:S(2)}, u32[]{:S(2)}) collective-permute-start(f32[2,96,128]{2,1,0:T(8,128)S(1)} %bitcast.46), channel_id=1, source_target_pairs={{0,4},{1,13},{2,6},{3,15},{4,8},{5,1},{6,10},{7,3},{8,12},{9,5},{1... | collective-permute-start | bytes 294920 | tf_op jit(solution)/shard_map/ppermute | solution.py:174
  69.1 8.1 %collective-permute-start.20 = (f32[2,96,128]{2,1,0:T(8,128)S(1)}, f32[2,96,128]{2,1,0:T(8,128)S(1)}, u32[]{:S(2)}, u32[]{:S(2)}) collective-permute-start(f32[2,96,128]{2,1,0:T(8,128)S(1)} %bitcast.44), channel_id=1, source_target_pairs={{0,2},{1,15},{2,4},{3,1},{4,6},{5,3},{6,8},{7,5},{8,10},{9,7},{10,... | collective-permute-start | bytes 294920 | tf_op jit(solution)/shard_map/ppermute | solution.py:174
  69.5 8.4 %collective-permute-start.19 = (f32[96,128]{1,0:T(8,128)S(1)}, f32[96,128]{1,0:T(8,128)S(1)}, u32[]{:S(2)}, u32[]{:S(2)}) collective-permute-start(f32[96,128]{1,0:T(8,128)S(1)} %slice.96), channel_id=1, source_target_pairs={{0,8},{1,9},{2,10},{3,11},{4,12},{5,13},{6,14},{7,15},{8,0},{9,1},... | collective-permute-start | bytes 147464 | tf_op jit(solution)/shard_map/ppermute | solution.py:175
  77.2 1.5 %collective-permute-start.23 = (f32[96,128]{1,0:T(8,128)S(1)}, f32[96,128]{1,0:T(8,128)S(1)}, u32[]{:S(2)}, u32[]{:S(2)}) collective-permute-start(f32[96,128]{1,0:T(8,128)S(1)} %fusion.6), channel_id=1, source_target_pairs={{0,1},{1,0},{2,3},{3,2},{4,5},{5,4},{6,7},{7,6},{8,9},{9,8},{10,11... | collective-permute-start | bytes 147464 | tf_op jit(solution)/shard_map/ppermute | solution.py:180

commit v4 on v3

--- a/solution.py
+++ b/solution.py
@@ -15,7 +15,7 @@
 SMALL_LIMIT = 10 * 2**20
 
 
-def split_kernel(slot_ref, source_ref, matrix_hbm, high_ref, low_ref, matrix_ref, sems, *, piece, first):
+def split_kernel(slot_ref, source_ref, matrix_hbm, parts_ref, matrix_ref, sems, *, piece, first):
     count = matrix_ref.shape[0] // piece
     owners = matrix_ref.shape[1] // piece
     width = ROUND * piece
@@ -35,9 +35,10 @@
         for k in range(ROUND):
             rows = turned[k * piece : (k + 1) * piece]
             high = rows.astype(jnp.bfloat16)
-            at = pl.ds(pl.multiple_of(slot_ref[j * ROUND + k] * piece, piece), piece)
-            high_ref[at, cols] = high
-            low_ref[at, cols] = (rows - high.astype(jnp.float32)).astype(jnp.bfloat16)
+            start = pl.multiple_of(slot_ref[j * ROUND + k] * piece, piece)
+            parts_ref[pl.ds(start, piece), cols] = high
+            below = pl.multiple_of(start + owners * piece // 2, piece)
+            parts_ref[pl.ds(below, piece), cols] = (rows - high.astype(jnp.float32)).astype(jnp.bfloat16)
 
 
 def split_matrix(slots, sources, columns, piece, first, count):
@@ -45,12 +46,12 @@
     depth = count * piece
     scalars = pl.BlockSpec(memory_space=pltpu.SMEM)
     on_chip = pl.BlockSpec(memory_space=pltpu.VMEM)
-    out = pltpu.VMEM((rows, depth), jnp.bfloat16)
+    out = pltpu.VMEM((2 * rows, depth), jnp.bfloat16)
     return pl.pallas_call(
         functools.partial(split_kernel, piece=piece, first=first),
         in_specs=[scalars, scalars, pl.BlockSpec(memory_space=pltpu.HBM)],
-        out_specs=[on_chip, on_chip],
-        out_shape=[out, out],
+        out_specs=[on_chip],
+        out_shape=[out],
         scratch_shapes=[pltpu.VMEM((depth, rows), jnp.float32), pltpu.SemaphoreType.DMA((count,))],
         compiler_params=pltpu.CompilerParams(vmem_limit_bytes=VMEM_LIMIT),
         name="split_matrix",
@@ -79,9 +80,9 @@
 
 
 def product_kernel(*refs, half, parts):
-    matrix, vectors, out_ref = refs[: 2 * parts], refs[2 * parts : -1], refs[-1]
+    matrix, vectors, out_ref = refs[:parts], refs[parts:-1], refs[-1]
     rows, width = out_ref.shape
-    at = pl.ds(half * rows, rows)
+    at = pl.ds(half * 2 * rows, 2 * rows)
     each = len(vectors) // parts
     total = None
     for n in range(parts):
@@ -89,18 +90,18 @@
         top = part.astype(jnp.bfloat16)
         rest = (part - top.astype(jnp.float32)).astype(jnp.bfloat16)
         both = jnp.concatenate([top, rest], axis=1)
-        main = jnp.dot(matrix[2 * n][at, :], both, preferred_element_type=jnp.float32)
-        small = jnp.dot(matrix[2 * n + 1][at, :], top, preferred_element_type=jnp.float32)
-        part_sum = main[:, :width] + (main[:, width:] + small)
+        four = jnp.dot(matrix[n][at, :], both, preferred_element_type=jnp.float32)
+        main, small = four[:rows], four[rows:]
+        part_sum = main[:, :width] + (main[:, width:] + (small[:, :width] + small[:, width:]))
         total = part_sum if total is None else total + part_sum
     out_ref[...] = total
 
 
 def product(matrix, vectors, half):
-    rows = matrix[0].shape[0] // 2
+    rows = matrix[0].shape[0] // 4
     on_chip = pl.BlockSpec(memory_space=pltpu.VMEM)
     return pl.pallas_call(
-        functools.partial(product_kernel, half=half, parts=len(matrix) // 2),
+        functools.partial(product_kernel, half=half, parts=len(matrix)),
         in_specs=[on_chip] * (len(matrix) + len(vectors)),
         out_specs=on_chip,
         out_shape=jax.ShapeDtypeStruct((rows, vectors[0].shape[1]), jnp.float32),
@@ -152,7 +153,7 @@
     shared = (ahead == 0) | (ahead == half)
     handler = jnp.where(shared, owner_core, before.astype(jnp.int32))
     slot = jnp.where(shared, jnp.where(ahead == 0, ring - 1, ring - 2), 2 * (hops - 1) + owner_core)
-    return (jnp.where(handler == core, 0, ring) + slot).astype(jnp.int32)
+    return (jnp.where(handler == core, 0, 2 * ring) + slot).astype(jnp.int32)
 
 
 SWAP = [(0, 1), (1, 0)]
@@ -195,7 +196,7 @@
     results = []
     for step in range(2):
         gathered = second_round(bundle(part, others))
-        for n in range(len(matrix) // 2, PARTS):
+        for n in range(len(matrix), PARTS):
             matrix = matrix + list(split_matrix(slots, order, columns, piece, n * count, count))
         theirs = product(matrix, gathered, 1)
         ours = product(matrix, gathered, 0)

time: 79.5 us -> 80.1 us (level)
  no operation moved by 1% of the time
where the time goes in v4:
time: 80.1 us; the launch traced here: 79.9 us
  starting transfers between devices  44.3 us (55%)
  waiting for transfers between devices  22.2 us (28%)
  Pallas kernels  10.9 us (14%)
  local copies, waits for them, and re-layouts  0.89 us (1%)
  other arithmetic  0.83 us (1%)
  between operations  0.81 us (1%)
    ppermute x6, starting transfers between devices, to_owners(): lax.ppermute(summed[2 * (hops - 1):2 * hops], axes, pairs(hops))  11.3 us
    ppermute x2, starting transfers between devices, to_owners(): opposite = lax.ppermute(summed[ring - 2], axes, pairs(half))  8.23 us
    ppermute x6, starting transfers between devices, first_round(): lax.ppermute(part, ('row', 'depth'), gather_pairs(True, shift))  7.92 us
    ppermute x2, starting transfers between devices, to_owners(): received = lax.ppermute(theirs, 'depth', SWAP)  7.4 us
    ppermute x6, waiting for transfers between devices, to_owners(): lax.ppermute(summed[2 * (hops - 1):2 * hops], axes, pairs(hops))  7.01 us
    ppermute x6, waiting for transfers between devices, first_round(): lax.ppermute(part, ('row', 'depth'), gather_pairs(True, shift))  6.72 us
    ppermute x6, waiting for transfers between devices, second_round(): lax.ppermute(line, ('row', 'depth'), gather_pairs(False, shift))  6.66 us
    ppermute x6, starting transfers between devices, second_round(): lax.ppermute(line, ('row', 'depth'), gather_pairs(False, shift))  6.16 us
  transfers between devices with their start and end apart: 24, of which 12 were waited for; matrix products, arithmetic and copies ran while one was open for 0% of the time, Pallas kernels for 10%

profile of v4, /device:TPU:1, one launch (start us, length us, event | category | flops | bytes accessed | tf_op | source)
XLA Modules:
  0.0 79.9 jit_solution(2356803245152085784)
XLA Ops:
  0.6 3.8 %collective-permute-start.2 = (f32[96,128]{1,0:T(8,128)}, f32[96,128]{1,0:T(8,128)S(1)}, u32[]{:S(2)}, u32[]{:S(2)}) collective-permute-start(f32[96,128]{1,0:T(8,128)} %bitcast.38), channel_id=1, source_target_pairs={{0,32},{1,129},{16,48},{17,145},{32,0},{33,161},{48,16},{49,177},{... | collective-permute-start | bytes 147464 | tf_op jit(solution)/shard_map/ppermute | solution.py:125
  4.5 0.8 collective-permute-start.1
  5.2 0.7 collective-permute-start
  5.9 0.0 copy-start.1
  5.9 0.8 %copy-done.1 = f32[1,1,96,128]{3,2,1,0:T(8,128)S(1)} copy-done((f32[1,1,96,128]{3,2,1,0:T(8,128)S(1)}, f32[1,1,96,128]{3,2,1,0:T(8,128)}, u32[]{:S(2)}) %copy-start.1) | copy-done | bytes 49176
  6.8 0.0 collective-permute-done.2.refs_3_
  6.8 0.8 %collective-permute-done.1.refs_2_ = f32[96,128]{1,0:T(8,128)S(1)} collective-permute-done((f32[96,128]{1,0:T(8,128)}, f32[96,128]{1,0:T(8,128)S(1)}, u32[]{:S(2)}, u32[]{:S(2)}) %collective-permute-start.1) | collective-permute-done | bytes 49184 | tf_op jit(solution)/shard_map/ppermute | solution.py:125
  7.6 2.0 %collective-permute-done.refs_1_ = f32[96,128]{1,0:T(8,128)S(1)} collective-permute-done((f32[96,128]{1,0:T(8,128)}, f32[96,128]{1,0:T(8,128)S(1)}, u32[]{:S(2)}, u32[]{:S(2)}) %collective-permute-start) | collective-permute-done | bytes 49184 | tf_op jit(solution)/shard_map/ppermute | solution.py:125
  9.6 2.8 %collective-permute-start.5 = (f32[384,128]{1,0:T(8,128)S(1)}, f32[384,128]{1,0:T(8,128)S(1)}, u32[]{:S(2)}, u32[]{:S(2)}) collective-permute-start(f32[384,128]{1,0:T(8,128)S(1)} %bundle.2.refs_1_), channel_id=1, source_target_pairs={{0,128},{1,33},{16,144},{17,49},{32,160},{33,1},{48,176},{49,17},{... | collective-permute-start | bytes 589832 | tf_op jit(solution)/shard_map/ppermute | solution.py:129
  12.4 0.9 %collective-permute-start.4 = (f32[384,128]{1,0:T(8,128)S(1)}, f32[384,128]{1,0:T(8,128)S(1)}, u32[]{:S(2)}, u32[]{:S(2)}) collective-permute-start(f32[384,128]{1,0:T(8,128)S(1)} %bundle.2.refs_1_), channel_id=1, source_target_pairs={{0,192},{1,49},{16,208},{17,1},{32,224},{33,17},{48,240},{49,33},{... | collective-permute-start | bytes 589832 | tf_op jit(solution)/shard_map/ppermute | solution.py:129
  13.3 0.6 collective-permute-start.3
  13.9 5.3 %split_matrix.1.refs_0_ = bf16[3072,1536]{1,0:T(8,128)(2,1)S(1)} custom-call(s32[16]{0:T(128)S(1)} %get-tuple-element.5.slot_ref, s32[16]{0:T(128)S(1)} %get-tuple-element.6.source_ref, f32[1536,1536]{1,0:T(8,128)} %bitcast.42), custom_call_target="tpu_custom_call" | custom-call | tf_op jit(solution)/shard_map/split_matrix/pallas_call | solution.py:50
  19.3 0.0 collective-permute-done.5.refs_4_
  19.3 0.0 collective-permute-done.4.refs_3_
  19.3 0.0 collective-permute-done.3.refs_2_
  19.3 1.4 %product.5 = f32[768,128]{1,0:T(8,128)S(1)} custom-call(bf16[3072,1536]{1,0:T(8,128)(2,1)S(1)} %split_matrix.1.refs_0_, f32[384,128]{1,0:T(8,128)S(1)} %bundle.2.refs_1_, f32[384,128]{1,0:T(8,128)S(1)} %collective-permute-done.3.refs_2_, f32[384,128]{1,0:T(8,128)S(1)} %collective-permute-done.4.refs_3_, f32[384,128]{1,0:T(8,128)S(1)} %collective-permute-done.5.refs_4_), custom_call_target="tpu_custom_call" | custom-call | tf_op jit(solution)/shard_map/product/pallas_call | solution.py:103
  20.7 3.9 %collective-permute-start.6 = (f32[768,128]{1,0:T(8,128)S(1)}, f32[768,128]{1,0:T(8,128)S(1)}, u32[]{:S(2)}, u32[]{:S(2)}) collective-permute-start(f32[768,128]{1,0:T(8,128)S(1)} %product.5), channel_id=1, source_target_pairs={{0,1},{1,0},{2,3},{3,2},{4,5},{5,4},{6,7},{7,6},{8,9},{9,8},{10,11... | collective-permute-start | bytes 1179656 | tf_op jit(solution)/shard_map/ppermute | solution.py:165
  24.6 1.4 %product.4 = f32[768,128]{1,0:T(8,128)S(1)} custom-call(bf16[3072,1536]{1,0:T(8,128)(2,1)S(1)} %split_matrix.1.refs_0_, f32[384,128]{1,0:T(8,128)S(1)} %bundle.2.refs_1_, f32[384,128]{1,0:T(8,128)S(1)} %collective-permute-done.3.refs_2_, f32[384,128]{1,0:T(8,128)S(1)} %collective-permute-done.4.refs_3_, f32[384,128]{1,0:T(8,128)S(1)} %collective-permute-done.5.refs_4_), custom_call_target="tpu_custom_call" | custom-call | tf_op jit(solution)/shard_map/product/pallas_call | solution.py:103
  26.0 0.0 collective-permute-done.6
  26.0 0.1 add.74
  26.1 6.5 %collective-permute-start.10 = (f32[2,96,128]{2,1,0:T(8,128)S(1)}, f32[2,96,128]{2,1,0:T(8,128)S(1)}, u32[]{:S(2)}, u32[]{:S(2)}) collective-permute-start(f32[2,96,128]{2,1,0:T(8,128)S(1)} %bitcast.47), channel_id=1, source_target_pairs={{0,6},{1,11},{2,8},{3,13},{4,10},{5,15},{6,12},{7,1},{8,14},{9,3},... | collective-permute-start | bytes 294920 | tf_op jit(solution)/shard_map/ppermute | solution.py:175
  32.7 0.3 collective-permute-start.9
  32.9 0.5 collective-permute-start.8
  33.4 4.6 %collective-permute-start.7 = (f32[96,128]{1,0:T(8,128)S(1)}, f32[96,128]{1,0:T(8,128)S(1)}, u32[]{:S(2)}, u32[]{:S(2)}) collective-permute-start(f32[96,128]{1,0:T(8,128)S(1)} %slice.89), channel_id=1, source_target_pairs={{0,8},{1,9},{2,10},{3,11},{4,12},{5,13},{6,14},{7,15},{8,0},{9,1},... | collective-permute-start | bytes 147464 | tf_op jit(solution)/shard_map/ppermute | solution.py:176
  38.0 0.0 collective-permute-done.10
  38.0 0.9 %collective-permute-done.9 = f32[2,96,128]{2,1,0:T(8,128)S(1)} collective-permute-done((f32[2,96,128]{2,1,0:T(8,128)S(1)}, f32[2,96,128]{2,1,0:T(8,128)S(1)}, u32[]{:S(2)}, u32[]{:S(2)}) %collective-permute-start.9) | collective-permute-done | bytes 98336 | tf_op jit(solution)/shard_map/ppermute | solution.py:175
  38.9 2.2 %collective-permute-done.8 = f32[2,96,128]{2,1,0:T(8,128)S(1)} collective-permute-done((f32[2,96,128]{2,1,0:T(8,128)S(1)}, f32[2,96,128]{2,1,0:T(8,128)S(1)}, u32[]{:S(2)}, u32[]{:S(2)}) %collective-permute-start.8) | collective-permute-done | bytes 98336 | tf_op jit(solution)/shard_map/ppermute | solution.py:175
  41.1 2.2 %collective-permute-start.11 = (f32[96,128]{1,0:T(8,128)S(1)}, f32[96,128]{1,0:T(8,128)S(1)}, u32[]{:S(2)}, u32[]{:S(2)}) collective-permute-start(f32[96,128]{1,0:T(8,128)S(1)} %fusion.5), channel_id=1, source_target_pairs={{0,1},{1,0},{2,3},{3,2},{4,5},{5,4},{6,7},{7,6},{8,9},{9,8},{10,11... | collective-permute-start | bytes 147464 | tf_op jit(solution)/shard_map/ppermute | solution.py:181
  43.3 0.0 collective-permute-done.7
  43.3 0.9 %collective-permute-done.11 = f32[96,128]{1,0:T(8,128)S(1)} collective-permute-done((f32[96,128]{1,0:T(8,128)S(1)}, f32[96,128]{1,0:T(8,128)S(1)}, u32[]{:S(2)}, u32[]{:S(2)}) %collective-permute-start.11) | collective-permute-done | bytes 49184 | tf_op jit(solution)/shard_map/ppermute | solution.py:181
  44.2 0.0 copy-start
  44.2 1.2 %collective-permute-start.14 = (f32[96,128]{1,0:T(8,128)S(1)}, f32[96,128]{1,0:T(8,128)S(1)}, u32[]{:S(2)}, u32[]{:S(2)}) collective-permute-start(f32[96,128]{1,0:T(8,128)S(1)} %fusion.4.refs_0_), channel_id=1, source_target_pairs={{0,32},{1,129},{16,48},{17,145},{32,0},{33,161},{48,16},{49,177},{... | collective-permute-start | bytes 147464 | tf_op jit(solution)/shard_map/ppermute | solution.py:125
  45.4 1.2 %collective-permute-start.13 = (f32[96,128]{1,0:T(8,128)S(1)}, f32[96,128]{1,0:T(8,128)S(1)}, u32[]{:S(2)}, u32[]{:S(2)}) collective-permute-start(f32[96,128]{1,0:T(8,128)S(1)} %fusion.4.refs_0_), channel_id=1, source_target_pairs={{0,48},{1,193},{16,0},{17,209},{32,16},{33,225},{48,32},{49,241},{... | collective-permute-start | bytes 147464 | tf_op jit(solution)/shard_map/ppermute | solution.py:125
  46.6 0.3 collective-permute-start.12
  46.9 1.9 %collective-permute-done.14.refs_3_ = f32[96,128]{1,0:T(8,128)S(1)} collective-permute-done((f32[96,128]{1,0:T(8,128)S(1)}, f32[96,128]{1,0:T(8,128)S(1)}, u32[]{:S(2)}, u32[]{:S(2)}) %collective-permute-start.14) | collective-permute-done | bytes 49184 | tf_op jit(solution)/shard_map/ppermute | solution.py:125
  48.8 0.0 collective-permute-done.13.refs_2_
  48.8 2.0 %collective-permute-done.12.refs_1_ = f32[96,128]{1,0:T(8,128)S(1)} collective-permute-done((f32[96,128]{1,0:T(8,128)S(1)}, f32[96,128]{1,0:T(8,128)S(1)}, u32[]{:S(2)}, u32[]{:S(2)}) %collective-permute-start.12) | collective-permute-done | bytes 49184 | tf_op jit(solution)/shard_map/ppermute | solution.py:125
  50.8 0.1 collective-permute-start.17
  50.9 1.8 %collective-permute-start.16 = (f32[384,128]{1,0:T(8,128)S(1)}, f32[384,128]{1,0:T(8,128)S(1)}, u32[]{:S(2)}, u32[]{:S(2)}) collective-permute-start(f32[384,128]{1,0:T(8,128)S(1)} %bundle.3.refs_1_), channel_id=1, source_target_pairs={{0,192},{1,49},{16,208},{17,1},{32,224},{33,17},{48,240},{49,33},{... | collective-permute-start | bytes 589832 | tf_op jit(solution)/shard_map/ppermute | solution.py:129
  52.6 0.0 collective-permute-start.15
  52.6 4.3 %collective-permute-done.17.refs_4_ = f32[384,128]{1,0:T(8,128)S(1)} collective-permute-done((f32[384,128]{1,0:T(8,128)S(1)}, f32[384,128]{1,0:T(8,128)S(1)}, u32[]{:S(2)}, u32[]{:S(2)}) %collective-permute-start.17) | collective-permute-done | bytes 196640 | tf_op jit(solution)/shard_map/ppermute | solution.py:129
  57.0 0.0 collective-permute-done.16.refs_3_
  57.0 2.3 %collective-permute-done.15.refs_2_ = f32[384,128]{1,0:T(8,128)S(1)} collective-permute-done((f32[384,128]{1,0:T(8,128)S(1)}, f32[384,128]{1,0:T(8,128)S(1)}, u32[]{:S(2)}, u32[]{:S(2)}) %collective-permute-start.15) | collective-permute-done | bytes 196640 | tf_op jit(solution)/shard_map/ppermute | solution.py:129
  59.3 1.4 %product.7 = f32[768,128]{1,0:T(8,128)S(1)} custom-call(bf16[3072,1536]{1,0:T(8,128)(2,1)S(1)} %split_matrix.1.refs_0_, f32[384,128]{1,0:T(8,128)S(1)} %bundle.3.refs_1_, f32[384,128]{1,0:T(8,128)S(1)} %collective-permute-done.15.refs_2_, f32[384,128]{1,0:T(8,128)S(1)} %collective-permute-done.16.refs_3_, f32[384,128]{1,0:T(8,128)S(1)} %collective-permute-done.17.refs_4_), custom_call_target="tpu_custom_call" | custom-call | tf_op jit(solution)/shard_map/product/pallas_call | solution.py:103
  60.7 3.5 %collective-permute-start.18 = (f32[768,128]{1,0:T(8,128)S(1)}, f32[768,128]{1,0:T(8,128)S(1)}, u32[]{:S(2)}, u32[]{:S(2)}) collective-permute-start(f32[768,128]{1,0:T(8,128)S(1)} %product.7), channel_id=1, source_target_pairs={{0,1},{1,0},{2,3},{3,2},{4,5},{5,4},{6,7},{7,6},{8,9},{9,8},{10,11... | collective-permute-start | bytes 1179656 | tf_op jit(solution)/shard_map/ppermute | solution.py:165
  64.2 1.4 %product.6 = f32[768,128]{1,0:T(8,128)S(1)} custom-call(bf16[3072,1536]{1,0:T(8,128)(2,1)S(1)} %split_matrix.1.refs_0_, f32[384,128]{1,0:T(8,128)S(1)} %bundle.3.refs_1_, f32[384,128]{1,0:T(8,128)S(1)} %collective-permute-done.15.refs_2_, f32[384,128]{1,0:T(8,128)S(1)} %collective-permute-done.16.refs_3_, f32[384,128]{1,0:T(8,128)S(1)} %collective-permute-done.17.refs_4_), custom_call_target="tpu_custom_call" | custom-call | tf_op jit(solution)/shard_map/product/pallas_call | solution.py:103
  65.6 0.0 copy-done
  65.6 0.0 collective-permute-done.18
  65.7 1.4 %collective-permute-start.22 = (f32[2,96,128]{2,1,0:T(8,128)S(1)}, f32[2,96,128]{2,1,0:T(8,128)S(1)}, u32[]{:S(2)}, u32[]{:S(2)}) collective-permute-start(f32[2,96,128]{2,1,0:T(8,128)S(1)} %bitcast.48), channel_id=1, source_target_pairs={{0,6},{1,11},{2,8},{3,13},{4,10},{5,15},{6,12},{7,1},{8,14},{9,3},... | collective-permute-start | bytes 294920 | tf_op jit(solution)/shard_map/ppermute | solution.py:175
  67.1 1.8 %collective-permute-start.21 = (f32[2,96,128]{2,1,0:T(8,128)S(1)}, f32[2,96,128]{2,1,0:T(8,128)S(1)}, u32[]{:S(2)}, u32[]{:S(2)}) collective-permute-start(f32[2,96,128]{2,1,0:T(8,128)S(1)} %bitcast.46), channel_id=1, source_target_pairs={{0,4},{1,13},{2,6},{3,15},{4,8},{5,1},{6,10},{7,3},{8,12},{9,5},{1... | collective-permute-start | bytes 294920 | tf_op jit(solution)/shard_map/ppermute | solution.py:175
  68.9 0.9 %collective-permute-start.20 = (f32[2,96,128]{2,1,0:T(8,128)S(1)}, f32[2,96,128]{2,1,0:T(8,128)S(1)}, u32[]{:S(2)}, u32[]{:S(2)}) collective-permute-start(f32[2,96,128]{2,1,0:T(8,128)S(1)} %bitcast.44), channel_id=1, source_target_pairs={{0,2},{1,15},{2,4},{3,1},{4,6},{5,3},{6,8},{7,5},{8,10},{9,7},{10,... | collective-permute-start | bytes 294920 | tf_op jit(solution)/shard_map/ppermute | solution.py:175
  69.7 3.7 %collective-permute-start.19 = (f32[96,128]{1,0:T(8,128)S(1)}, f32[96,128]{1,0:T(8,128)S(1)}, u32[]{:S(2)}, u32[]{:S(2)}) collective-permute-start(f32[96,128]{1,0:T(8,128)S(1)} %slice.96), channel_id=1, source_target_pairs={{0,8},{1,9},{2,10},{3,11},{4,12},{5,13},{6,14},{7,15},{8,0},{9,1},... | collective-permute-start | bytes 147464 | tf_op jit(solution)/shard_map/ppermute | solution.py:176
  73.4 0.0 collective-permute-done.22
  73.4 1.7 %collective-permute-done.21 = f32[2,96,128]{2,1,0:T(8,128)S(1)} collective-permute-done((f32[2,96,128]{2,1,0:T(8,128)S(1)}, f32[2,96,128]{2,1,0:T(8,128)S(1)}, u32[]{:S(2)}, u32[]{:S(2)}) %collective-permute-start.21) | collective-permute-done | bytes 98336 | tf_op jit(solution)/shard_map/ppermute | solution.py:175
  75.1 2.2 %collective-permute-done.20 = f32[2,96,128]{2,1,0:T(8,128)S(1)} collective-permute-done((f32[2,96,128]{2,1,0:T(8,128)S(1)}, f32[2,96,128]{2,1,0:T(8,128)S(1)}, u32[]{:S(2)}, u32[]{:S(2)}) %collective-permute-start.20) | collective-permute-done | bytes 98336 | tf_op jit(solution)/shard_map/ppermute | solution.py:175
  77.4 1.1 %collective-permute-start.23 = (f32[96,128]{1,0:T(8,128)S(1)}, f32[96,128]{1,0:T(8,128)S(1)}, u32[]{:S(2)}, u32[]{:S(2)}) collective-permute-start(f32[96,128]{1,0:T(8,128)S(1)} %fusion.6), channel_id=1, source_target_pairs={{0,1},{1,0},{2,3},{3,2},{4,5},{5,4},{6,7},{7,6},{8,9},{9,8},{10,11... | collective-permute-start | bytes 147464 | tf_op jit(solution)/shard_map/ppermute | solution.py:181
  78.4 0.0 collective-permute-done.19
  78.4 0.9 %collective-permute-done.23 = f32[96,128]{1,0:T(8,128)S(1)} collective-permute-done((f32[96,128]{1,0:T(8,128)S(1)}, f32[96,128]{1,0:T(8,128)S(1)}, u32[]{:S(2)}, u32[]{:S(2)}) %collective-permute-start.23) | collective-permute-done | bytes 49184 | tf_op jit(solution)/shard_map/ppermute | solution.py:181
  79.3 0.6 fusion.2
  (16 shorter events, 0.2 us)
Async XLA Ops:
  0.6 6.1 %collective-permute-start.2 = (f32[96,128]{1,0:T(8,128)}, f32[96,128]{1,0:T(8,128)S(1)}, u32[]{:S(2)}, u32[]{:S(2)}) collective-permute-start(f32[96,128]{1,0:T(8,128)} %bitcast.38), channel_id=1, source_target_pairs={{0,32},{1,129},{16,48},{17,145},{32,0},{33,161},{48,16},{49,177},{... | collective-permute-start | bytes 147464 | tf_op jit(solution)/shard_map/ppermute | solution.py:125
  4.5 3.2 %collective-permute-start.1 = (f32[96,128]{1,0:T(8,128)}, f32[96,128]{1,0:T(8,128)S(1)}, u32[]{:S(2)}, u32[]{:S(2)}) collective-permute-start(f32[96,128]{1,0:T(8,128)} %bitcast.39), channel_id=1, source_target_pairs={{0,48},{1,193},{16,0},{17,209},{32,16},{33,225},{48,32},{49,241},{... | collective-permute-start | bytes 147464 | tf_op jit(solution)/shard_map/ppermute | solution.py:125
  5.2 4.4 %collective-permute-start = (f32[96,128]{1,0:T(8,128)}, f32[96,128]{1,0:T(8,128)S(1)}, u32[]{:S(2)}, u32[]{:S(2)}) collective-permute-start(f32[96,128]{1,0:T(8,128)} %bitcast.40), channel_id=1, source_target_pairs={{0,16},{1,65},{16,32},{17,81},{32,48},{33,97},{48,0},{49,113},{64,... | collective-permute-start | bytes 147464 | tf_op jit(solution)/shard_map/ppermute | solution.py:125
  5.9 0.8 %copy-start.1 = (f32[1,1,96,128]{3,2,1,0:T(8,128)S(1)}, f32[1,1,96,128]{3,2,1,0:T(8,128)}, u32[]{:S(2)}) copy-start(f32[1,1,96,128]{3,2,1,0:T(8,128)} %param.3) | copy-start | bytes 147460
  9.6 9.7 %collective-permute-start.5 = (f32[384,128]{1,0:T(8,128)S(1)}, f32[384,128]{1,0:T(8,128)S(1)}, u32[]{:S(2)}, u32[]{:S(2)}) collective-permute-start(f32[384,128]{1,0:T(8,128)S(1)} %bundle.2.refs_1_), channel_id=1, source_target_pairs={{0,128},{1,33},{16,144},{17,49},{32,160},{33,1},{48,176},{49,17},{... | collective-permute-start | bytes 589832 | tf_op jit(solution)/shard_map/ppermute | solution.py:129
  12.4 6.8 %collective-permute-start.4 = (f32[384,128]{1,0:T(8,128)S(1)}, f32[384,128]{1,0:T(8,128)S(1)}, u32[]{:S(2)}, u32[]{:S(2)}) collective-permute-start(f32[384,128]{1,0:T(8,128)S(1)} %bundle.2.refs_1_), channel_id=1, source_target_pairs={{0,192},{1,49},{16,208},{17,1},{32,224},{33,17},{48,240},{49,33},{... | collective-permute-start | bytes 589832 | tf_op jit(solution)/shard_map/ppermute | solution.py:129
  13.3 6.0 %collective-permute-start.3 = (f32[384,128]{1,0:T(8,128)S(1)}, f32[384,128]{1,0:T(8,128)S(1)}, u32[]{:S(2)}, u32[]{:S(2)}) collective-permute-start(f32[384,128]{1,0:T(8,128)S(1)} %bundle.2.refs_1_), channel_id=1, source_target_pairs={{0,64},{1,17},{16,80},{17,33},{32,96},{33,49},{48,112},{49,1},{64,... | collective-permute-start | bytes 589832 | tf_op jit(solution)/shard_map/ppermute | solution.py:129
  20.7 5.3 %collective-permute-start.6 = (f32[768,128]{1,0:T(8,128)S(1)}, f32[768,128]{1,0:T(8,128)S(1)}, u32[]{:S(2)}, u32[]{:S(2)}) collective-permute-start(f32[768,128]{1,0:T(8,128)S(1)} %product.5), channel_id=1, source_target_pairs={{0,1},{1,0},{2,3},{3,2},{4,5},{5,4},{6,7},{7,6},{8,9},{9,8},{10,11... | collective-permute-start | bytes 1179656 | tf_op jit(solution)/shard_map/ppermute | solution.py:165
  26.1 11.9 %collective-permute-start.10 = (f32[2,96,128]{2,1,0:T(8,128)S(1)}, f32[2,96,128]{2,1,0:T(8,128)S(1)}, u32[]{:S(2)}, u32[]{:S(2)}) collective-permute-start(f32[2,96,128]{2,1,0:T(8,128)S(1)} %bitcast.47), channel_id=1, source_target_pairs={{0,6},{1,11},{2,8},{3,13},{4,10},{5,15},{6,12},{7,1},{8,14},{9,3},... | collective-permute-start | bytes 294920 | tf_op jit(solution)/shard_map/ppermute | solution.py:175
  32.7 6.2 %collective-permute-start.9 = (f32[2,96,128]{2,1,0:T(8,128)S(1)}, f32[2,96,128]{2,1,0:T(8,128)S(1)}, u32[]{:S(2)}, u32[]{:S(2)}) collective-permute-start(f32[2,96,128]{2,1,0:T(8,128)S(1)} %bitcast.45), channel_id=1, source_target_pairs={{0,4},{1,13},{2,6},{3,15},{4,8},{5,1},{6,10},{7,3},{8,12},{9,5},{1... | collective-permute-start | bytes 294920 | tf_op jit(solution)/shard_map/ppermute | solution.py:175
  32.9 8.1 %collective-permute-start.8 = (f32[2,96,128]{2,1,0:T(8,128)S(1)}, f32[2,96,128]{2,1,0:T(8,128)S(1)}, u32[]{:S(2)}, u32[]{:S(2)}) collective-permute-start(f32[2,96,128]{2,1,0:T(8,128)S(1)} %bitcast.43), channel_id=1, source_target_pairs={{0,2},{1,15},{2,4},{3,1},{4,6},{5,3},{6,8},{7,5},{8,10},{9,7},{10,... | collective-permute-start | bytes 294920 | tf_op jit(solution)/shard_map/ppermute | solution.py:175
  33.4 9.9 %collective-permute-start.7 = (f32[96,128]{1,0:T(8,128)S(1)}, f32[96,128]{1,0:T(8,128)S(1)}, u32[]{:S(2)}, u32[]{:S(2)}) collective-permute-start(f32[96,128]{1,0:T(8,128)S(1)} %slice.89), channel_id=1, source_target_pairs={{0,8},{1,9},{2,10},{3,11},{4,12},{5,13},{6,14},{7,15},{8,0},{9,1},... | collective-permute-start | bytes 147464 | tf_op jit(solution)/shard_map/ppermute | solution.py:176
  41.1 3.1 %collective-permute-start.11 = (f32[96,128]{1,0:T(8,128)S(1)}, f32[96,128]{1,0:T(8,128)S(1)}, u32[]{:S(2)}, u32[]{:S(2)}) collective-permute-start(f32[96,128]{1,0:T(8,128)S(1)} %fusion.5), channel_id=1, source_target_pairs={{0,1},{1,0},{2,3},{3,2},{4,5},{5,4},{6,7},{7,6},{8,9},{9,8},{10,11... | collective-permute-start | bytes 147464 | tf_op jit(solution)/shard_map/ppermute | solution.py:181
  44.2 21.3 %copy-start = (f32[96,128]{1,0:T(8,128)}, f32[96,128]{1,0:T(8,128)S(1)}, u32[]{:S(2)}) copy-start(f32[96,128]{1,0:T(8,128)S(1)} %fusion.4.refs_0_) | copy-start | bytes 147460
  44.2 4.5 %collective-permute-start.14 = (f32[96,128]{1,0:T(8,128)S(1)}, f32[96,128]{1,0:T(8,128)S(1)}, u32[]{:S(2)}, u32[]{:S(2)}) collective-permute-start(f32[96,128]{1,0:T(8,128)S(1)} %fusion.4.refs_0_), channel_id=1, source_target_pairs={{0,32},{1,129},{16,48},{17,145},{32,0},{33,161},{48,16},{49,177},{... | collective-permute-start | bytes 147464 | tf_op jit(solution)/shard_map/ppermute | solution.py:125
  45.4 3.4 %collective-permute-start.13 = (f32[96,128]{1,0:T(8,128)S(1)}, f32[96,128]{1,0:T(8,128)S(1)}, u32[]{:S(2)}, u32[]{:S(2)}) collective-permute-start(f32[96,128]{1,0:T(8,128)S(1)} %fusion.4.refs_0_), channel_id=1, source_target_pairs={{0,48},{1,193},{16,0},{17,209},{32,16},{33,225},{48,32},{49,241},{... | collective-permute-start | bytes 147464 | tf_op jit(solution)/shard_map/ppermute | solution.py:125
  46.6 4.2 %collective-permute-start.12 = (f32[96,128]{1,0:T(8,128)S(1)}, f32[96,128]{1,0:T(8,128)S(1)}, u32[]{:S(2)}, u32[]{:S(2)}) collective-permute-start(f32[96,128]{1,0:T(8,128)S(1)} %fusion.4.refs_0_), channel_id=1, source_target_pairs={{0,16},{1,65},{16,32},{17,81},{32,48},{33,97},{48,0},{49,113},{64,... | collective-permute-start | bytes 147464 | tf_op jit(solution)/shard_map/ppermute | solution.py:125
  50.8 6.2 %collective-permute-start.17 = (f32[384,128]{1,0:T(8,128)S(1)}, f32[384,128]{1,0:T(8,128)S(1)}, u32[]{:S(2)}, u32[]{:S(2)}) collective-permute-start(f32[384,128]{1,0:T(8,128)S(1)} %bundle.3.refs_1_), channel_id=1, source_target_pairs={{0,128},{1,33},{16,144},{17,49},{32,160},{33,1},{48,176},{49,17},{... | collective-permute-start | bytes 589832 | tf_op jit(solution)/shard_map/ppermute | solution.py:129
  50.9 6.1 %collective-permute-start.16 = (f32[384,128]{1,0:T(8,128)S(1)}, f32[384,128]{1,0:T(8,128)S(1)}, u32[]{:S(2)}, u32[]{:S(2)}) collective-permute-start(f32[384,128]{1,0:T(8,128)S(1)} %bundle.3.refs_1_), channel_id=1, source_target_pairs={{0,192},{1,49},{16,208},{17,1},{32,224},{33,17},{48,240},{49,33},{... | collective-permute-start | bytes 589832 | tf_op jit(solution)/shard_map/ppermute | solution.py:129
  52.6 6.7 %collective-permute-start.15 = (f32[384,128]{1,0:T(8,128)S(1)}, f32[384,128]{1,0:T(8,128)S(1)}, u32[]{:S(2)}, u32[]{:S(2)}) collective-permute-start(f32[384,128]{1,0:T(8,128)S(1)} %bundle.3.refs_1_), channel_id=1, source_target_pairs={{0,64},{1,17},{16,80},{17,33},{32,96},{33,49},{48,112},{49,1},{64,... | collective-permute-start | bytes 589832 | tf_op jit(solution)/shard_map/ppermute | solution.py:129
  60.7 4.9 %collective-permute-start.18 = (f32[768,128]{1,0:T(8,128)S(1)}, f32[768,128]{1,0:T(8,128)S(1)}, u32[]{:S(2)}, u32[]{:S(2)}) collective-permute-start(f32[768,128]{1,0:T(8,128)S(1)} %product.7), channel_id=1, source_target_pairs={{0,1},{1,0},{2,3},{3,2},{4,5},{5,4},{6,7},{7,6},{8,9},{9,8},{10,11... | collective-permute-start | bytes 1179656 | tf_op jit(solution)/shard_map/ppermute | solution.py:165
  65.7 7.7 %collective-permute-start.22 = (f32[2,96,128]{2,1,0:T(8,128)S(1)}, f32[2,96,128]{2,1,0:T(8,128)S(1)}, u32[]{:S(2)}, u32[]{:S(2)}) collective-permute-start(f32[2,96,128]{2,1,0:T(8,128)S(1)} %bitcast.48), channel_id=1, source_target_pairs={{0,6},{1,11},{2,8},{3,13},{4,10},{5,15},{6,12},{7,1},{8,14},{9,3},... | collective-permute-start | bytes 294920 | tf_op jit(solution)/shard_map/ppermute | solution.py:175
  67.1 8.0 %collective-permute-start.21 = (f32[2,96,128]{2,1,0:T(8,128)S(1)}, f32[2,96,128]{2,1,0:T(8,128)S(1)}, u32[]{:S(2)}, u32[]{:S(2)}) collective-permute-start(f32[2,96,128]{2,1,0:T(8,128)S(1)} %bitcast.46), channel_id=1, source_target_pairs={{0,4},{1,13},{2,6},{3,15},{4,8},{5,1},{6,10},{7,3},{8,12},{9,5},{1... | collective-permute-start | bytes 294920 | tf_op jit(solution)/shard_map/ppermute | solution.py:175
  68.9 8.4 %collective-permute-start.20 = (f32[2,96,128]{2,1,0:T(8,128)S(1)}, f32[2,96,128]{2,1,0:T(8,128)S(1)}, u32[]{:S(2)}, u32[]{:S(2)}) collective-permute-start(f32[2,96,128]{2,1,0:T(8,128)S(1)} %bitcast.44), channel_id=1, source_target_pairs={{0,2},{1,15},{2,4},{3,1},{4,6},{5,3},{6,8},{7,5},{8,10},{9,7},{10,... | collective-permute-start | bytes 294920 | tf_op jit(solution)/shard_map/ppermute | solution.py:175
  69.7 8.7 %collective-permute-start.19 = (f32[96,128]{1,0:T(8,128)S(1)}, f32[96,128]{1,0:T(8,128)S(1)}, u32[]{:S(2)}, u32[]{:S(2)}) collective-permute-start(f32[96,128]{1,0:T(8,128)S(1)} %slice.96), channel_id=1, source_target_pairs={{0,8},{1,9},{2,10},{3,11},{4,12},{5,13},{6,14},{7,15},{8,0},{9,1},... | collective-permute-start | bytes 147464 | tf_op jit(solution)/shard_map/ppermute | solution.py:176
  77.4 1.9 %collective-permute-start.23 = (f32[96,128]{1,0:T(8,128)S(1)}, f32[96,128]{1,0:T(8,128)S(1)}, u32[]{:S(2)}, u32[]{:S(2)}) collective-permute-start(f32[96,128]{1,0:T(8,128)S(1)} %fusion.6), channel_id=1, source_target_pairs={{0,1},{1,0},{2,3},{3,2},{4,5},{5,4},{6,7},{7,6},{8,9},{9,8},{10,11... | collective-permute-start | bytes 147464 | tf_op jit(solution)/shard_map/ppermute | solution.py:181
